TPU v7x, 256 devices: a whole 4x4x8 slice. The times are simulated.
256 devices in a mesh: tm: 64 (over z_hi, y, x), head: 4 (over z_lo, core).
Axes of the slice: x: 4, y: 4, z: 8 (z_hi: 4, z_lo: 2; z = z_hi * 2 + z_lo), core: 2. Of those that a mesh axis runs over, the one named last changes fastest.
Arguments:
- query: bfloat16 [16384, 4096], P('tm', 'head'), may hold values from -200 to 200
- key_in: bfloat16 [16384, 4096], P('tm', 'head'), may hold values from -7 to 7
- value: bfloat16 [16384, 4096], P('tm', 'head'), may hold values from -6 to 6
- grad_out: bfloat16 [16384, 4096], P('tm', 'head'), may hold values from -6 to 6
- weights: bfloat16 [3, 4096, 4096], P(None, 'tm', 'head'), may hold values from -0.09375 to 0.09375
Outputs:
- grad_input_t: bfloat16 [4096, 16384], P('head', 'tm')
All inputs are finite; a program needn't handle non-finite values.
Results may differ from a plain program's by a relative error of at most 0.0091.
Values may be sent and summed in bfloat16 or wider, within the bound.
A program may use at most 256 MiB of HBM per device.

v0:
```python
import jax
import jax.numpy as jnp
from jax import lax
from jax.sharding import PartitionSpec as P

HD = 128


def temporal(q_heads, k_heads, v_heads, g_heads):
    scale = 1.0 / q_heads.shape[-1] ** 0.5
    scores = (
        jnp.einsum("fphd,gphd->phfg", q_heads, k_heads, preferred_element_type=jnp.float32) * scale
    )
    probs = jax.nn.softmax(scores, axis=-1)
    probs_b = probs.astype(jnp.bfloat16)
    attended = jnp.einsum("phfg,gphd->fphd", probs_b, v_heads, preferred_element_type=jnp.float32)
    delta = jnp.transpose(jnp.sum(g_heads.astype(jnp.float32) * attended, axis=-1), (1, 2, 0))
    grad_probs = jnp.einsum("fphd,gphd->phfg", g_heads, v_heads, preferred_element_type=jnp.float32)
    grad_scores = (probs * (grad_probs - delta[..., None])).astype(jnp.bfloat16)
    grad_value = jnp.einsum("phfg,fphd->gphd", probs_b, g_heads, preferred_element_type=jnp.float32)
    grad_query = (
        jnp.einsum("phfg,gphd->fphd", grad_scores, k_heads, preferred_element_type=jnp.float32)
        * scale
    )
    grad_key = (
        jnp.einsum("phfg,fphd->gphd", grad_scores, q_heads, preferred_element_type=jnp.float32)
        * scale
    )
    return (
        grad_query.astype(jnp.bfloat16),
        grad_key.astype(jnp.bfloat16),
        grad_value.astype(jnp.bfloat16),
    )


def per_device(query, key_in, value, grad_out, weights):
    tok_rows, width = query.shape
    head_count = width // HD

    def split_heads(array):
        return array.reshape(1, tok_rows, head_count, HD)

    sq = split_heads(query)
    sk = split_heads(key_in)
    sv = split_heads(value)
    sg = split_heads(grad_out)
    moved = (
        lax.all_to_all(sq, "tm", split_axis=1, concat_axis=0, tiled=True),
        lax.all_to_all(sk, "tm", split_axis=1, concat_axis=0, tiled=True),
        lax.all_to_all(sv, "tm", split_axis=1, concat_axis=0, tiled=True),
        lax.all_to_all(sg, "tm", split_axis=1, concat_axis=0, tiled=True),
    )
    grads = temporal(moved[0], moved[1], moved[2], moved[3])
    back = (
        lax.all_to_all(grads[0], "tm", split_axis=0, concat_axis=1, tiled=True),
        lax.all_to_all(grads[1], "tm", split_axis=0, concat_axis=1, tiled=True),
        lax.all_to_all(grads[2], "tm", split_axis=0, concat_axis=1, tiled=True),
    )
    stacked = jnp.stack(
        [
            back[0].reshape(tok_rows, width),
            back[1].reshape(tok_rows, width),
            back[2].reshape(tok_rows, width),
        ]
    )
    partial_sum = jnp.einsum(
        "mic,mtc->it",
        lax.all_gather(weights, "tm", axis=1, tiled=True),
        stacked,
        preferred_element_type=jnp.float32,
    )
    mine = lax.psum_scatter(partial_sum, "head", scatter_dimension=0, tiled=True)
    return mine.astype(jnp.bfloat16)


def solution(mesh):
    placed = (
        P("tm", "head"),
        P("tm", "head"),
        P("tm", "head"),
        P("tm", "head"),
        P(None, "tm", "head"),
    )
    return jax.shard_map(
        per_device, mesh=mesh, in_specs=placed, out_specs=P("head", "tm"), check_vma=False
    )
```

profile of v0, /device:TPU:1, one launch (start us, length us, event | category | flops | bytes accessed | tf_op | source)
XLA Modules:
  0.0 372.9 jit_solution(12953759409687776059)
XLA Ops:
  6.5 0.7 all-gather.2.cloned.1.call-update
  7.3 2.0 copy.45
  9.2 15.1 %all-to-all-start = ((bf16[1,256,8,128]{3,2,0,1:T(8,128)(2,1)}), bf16[1,256,8,128]{3,2,0,1:T(8,128)(2,1)S(1)}, u32[]{:S(2)}, u32[]{:S(2)}) async-start(bf16[1,256,8,128]{3,2,0,1:T(8,128)(2,1)} %bitcast.15), calls=%async_computation | async-start | bytes 1048576 | tf_op jit(solution)/shard_map/all_to_all | solution.py:48
  24.3 1.9 copy.46
  26.3 17.0 %all-to-all-done = bf16[1,256,8,128]{3,2,0,1:T(8,128)(2,1)S(1)} async-done(((bf16[1,256,8,128]{3,2,0,1:T(8,128)(2,1)}), bf16[1,256,8,128]{3,2,0,1:T(8,128)(2,1)S(1)}, u32[]{:S(2)}, u32[]{:S(2)}) %all-to-all-start) | async-done | bytes 524320 | tf_op jit(solution)/shard_map/all_to_all | solution.py:48
  43.3 9.4 %all-to-all-start.1 = ((bf16[1,256,8,128]{3,2,0,1:T(8,128)(2,1)}), bf16[1,256,8,128]{3,2,0,1:T(8,128)(2,1)S(1)}, u32[]{:S(2)}, u32[]{:S(2)}) async-start(bf16[1,256,8,128]{3,2,0,1:T(8,128)(2,1)} %bitcast.19), calls=%async_computation.1 | async-start | bytes 1048576 | tf_op jit(solution)/shard_map/all_to_all | solution.py:49
  52.7 0.9 copy.48
  53.6 13.5 %all-to-all-done.1 = bf16[1,256,8,128]{3,2,0,1:T(8,128)(2,1)S(1)} async-done(((bf16[1,256,8,128]{3,2,0,1:T(8,128)(2,1)}), bf16[1,256,8,128]{3,2,0,1:T(8,128)(2,1)S(1)}, u32[]{:S(2)}, u32[]{:S(2)}) %all-to-all-start.1) | async-done | bytes 524320 | tf_op jit(solution)/shard_map/all_to_all | solution.py:49
  67.0 4.9 %all-to-all-start.3 = ((bf16[1,256,8,128]{3,2,0,1:T(8,128)(2,1)}), bf16[1,256,8,128]{3,2,0,1:T(8,128)(2,1)S(1)}, u32[]{:S(2)}, u32[]{:S(2)}) async-start(bf16[1,256,8,128]{3,2,0,1:T(8,128)(2,1)} %bitcast.27), calls=%async_computation.3 | async-start | bytes 1048576 | tf_op jit(solution)/shard_map/all_to_all | solution.py:50
  71.9 0.9 copy.47
  72.8 30.1 %all-to-all-done.3 = bf16[1,256,8,128]{3,2,0,1:T(8,128)(2,1)S(1)} async-done(((bf16[1,256,8,128]{3,2,0,1:T(8,128)(2,1)}), bf16[1,256,8,128]{3,2,0,1:T(8,128)(2,1)S(1)}, u32[]{:S(2)}, u32[]{:S(2)}) %all-to-all-start.3) | async-done | bytes 524320 | tf_op jit(solution)/shard_map/all_to_all | solution.py:50
  103.0 6.8 %all-to-all-start.2 = ((bf16[1,256,8,128]{3,2,0,1:T(8,128)(2,1)}), bf16[1,256,8,128]{3,2,0,1:T(8,128)(2,1)S(1)}, u32[]{:S(2)}, u32[]{:S(2)}) async-start(bf16[1,256,8,128]{3,2,0,1:T(8,128)(2,1)} %bitcast.23), calls=%async_computation.2 | async-start | bytes 1048576 | tf_op jit(solution)/shard_map/all_to_all | solution.py:51
  109.7 0.6 fusion.39
  110.4 13.6 %all-to-all-done.2 = bf16[1,256,8,128]{3,2,0,1:T(8,128)(2,1)S(1)} async-done(((bf16[1,256,8,128]{3,2,0,1:T(8,128)(2,1)}), bf16[1,256,8,128]{3,2,0,1:T(8,128)(2,1)S(1)}, u32[]{:S(2)}, u32[]{:S(2)}) %all-to-all-start.2) | async-done | bytes 524320 | tf_op jit(solution)/shard_map/all_to_all | solution.py:51
  124.0 0.6 fusion.13
  124.6 2.1 fusion.10
  127.0 1.1 copy.38
  128.2 5.9 %all-to-all-start.5 = ((bf16[64,4,8,128]{3,2,1,0:T(8,128)(2,1)}), bf16[64,4,8,128]{3,2,1,0:T(8,128)(2,1)S(1)}, u32[]{:S(2)}, u32[]{:S(2)}) async-start(bf16[64,4,8,128]{3,2,1,0:T(8,128)(2,1)} %copy.38), calls=%async_computation.5 | async-start | bytes 1048576 | tf_op jit(solution)/shard_map/all_to_all | solution.py:56
  134.1 0.4 fusion.15
  134.5 1.2 copy.36
  135.6 18.6 %all-to-all-done.5 = bf16[64,4,8,128]{3,2,1,0:T(8,128)(2,1)S(1)} async-done(((bf16[64,4,8,128]{3,2,1,0:T(8,128)(2,1)}), bf16[64,4,8,128]{3,2,1,0:T(8,128)(2,1)S(1)}, u32[]{:S(2)}, u32[]{:S(2)}) %all-to-all-start.5) | async-done | bytes 524320 | tf_op jit(solution)/shard_map/all_to_all | solution.py:56
  154.3 11.3 %all-to-all-start.4 = ((bf16[64,4,8,128]{3,2,1,0:T(8,128)(2,1)}), bf16[64,4,8,128]{3,2,1,0:T(8,128)(2,1)S(1)}, u32[]{:S(2)}, u32[]{:S(2)}) async-start(bf16[64,4,8,128]{3,2,1,0:T(8,128)(2,1)} %copy.36), calls=%async_computation.4 | async-start | bytes 1048576 | tf_op jit(solution)/shard_map/all_to_all | solution.py:55
  165.6 1.6 fusion.16
  167.2 1.1 copy.40
  168.3 17.4 %all-to-all-done.4 = bf16[64,4,8,128]{3,2,1,0:T(8,128)(2,1)S(1)} async-done(((bf16[64,4,8,128]{3,2,1,0:T(8,128)(2,1)}), bf16[64,4,8,128]{3,2,1,0:T(8,128)(2,1)S(1)}, u32[]{:S(2)}, u32[]{:S(2)}) %all-to-all-start.4) | async-done | bytes 524320 | tf_op jit(solution)/shard_map/all_to_all | solution.py:55
  185.7 6.5 %all-to-all-start.6 = ((bf16[64,4,8,128]{3,2,1,0:T(8,128)(2,1)}), bf16[64,4,8,128]{3,2,1,0:T(8,128)(2,1)S(1)}, u32[]{:S(2)}, u32[]{:S(2)}) async-start(bf16[64,4,8,128]{3,2,1,0:T(8,128)(2,1)} %copy.40), calls=%async_computation.6 | async-start | bytes 1048576 | tf_op jit(solution)/shard_map/all_to_all | solution.py:57
  193.0 19.5 %all-to-all-done.6 = bf16[64,4,8,128]{3,2,1,0:T(8,128)(2,1)S(1)} async-done(((bf16[64,4,8,128]{3,2,1,0:T(8,128)(2,1)}), bf16[64,4,8,128]{3,2,1,0:T(8,128)(2,1)S(1)}, u32[]{:S(2)}, u32[]{:S(2)}) %all-to-all-start.6) | async-done | bytes 524320 | tf_op jit(solution)/shard_map/all_to_all | solution.py:57
  212.7 24.6 %all-gather.2.cloned.1.call-done = bf16[3,4096,1024]{2,1,0:T(8,128)(2,1)} async-done(((bf16[3,64,1024]{2,1,0:T(8,128)(2,1)}), bf16[3,4096,1024]{2,1,0:T(8,128)(2,1)}) %all-gather.2.cloned.1.call-update) | async-done | bytes 25165840 | tf_op jit(solution)/shard_map/all_gather | solution.py:68
  237.3 13.8 %convolution_bitcast_fusion = f32[4096,256]{0,1:T(8,128)} fusion(bf16[3,4096,1024]{2,1,0:T(8,128)(2,1)} %all-gather.2.cloned.1.call-done, bf16[1,256,1024]{2,1,0:T(8,128)(2,1)S(1)} %stack_reshape.11, bf16[1,256,1024]{2,1,0:T(8,128)(2,1)S(1)} %stack_reshape.10, bf16[1,256,1024]{2,1,0:T(8,128)(2,1)S(1)} %stack_reshape.9), kind=kOutput, calls=%fused_computation.1 | convolution fusion | flops 6444023808 | bytes 30932992 | tf_op jit(solution)/shard_map/mic,mtc->it/dot_general | solution.py:66
  251.1 112.7 %reduce-scatter.2.cloned.1.call-done = f32[1024,256]{0,1:T(8,128)} async-done(((f32[4096,256]{0,1:T(8,128)}), f32[1024,256]{0,1:T(8,128)}) %reduce-scatter.2.cloned.1.call-update) | async-done | bytes 1048592 | tf_op jit(solution)/shard_map/reduce_scatter | solution.py:72
  363.8 1.3 convert_element_type.39
  365.1 1.0 copy.41
  (13 shorter events, 1.3 us)
Async XLA Ops:
  6.5 46.1 %copy-start = (bf16[256,1024]{1,0:T(8,128)(2,1)S(1)}, bf16[256,1024]{1,0:T(8,128)(2,1)}, u32[]{:S(2)}) copy-start(bf16[256,1024]{1,0:T(8,128)(2,1)} %param.7) | copy-start | bytes 1572868
  6.5 65.4 %copy-start.1 = (bf16[256,1024]{1,0:T(8,128)(2,1)S(1)}, bf16[256,1024]{1,0:T(8,128)(2,1)}, u32[]{:S(2)}) copy-start(bf16[256,1024]{1,0:T(8,128)(2,1)} %param.8) | copy-start | bytes 1572868
  6.5 230.8 %all-gather.2.cloned.1.call-start = ((), (), s32[]{:S(2)}) async-start(), calls=%async_computation.8 | async-start | bytes 25559040 | tf_op jit(solution)/shard_map/all_gather | solution.py:68
  9.2 34.0 %all-to-all-start = ((bf16[1,256,8,128]{3,2,0,1:T(8,128)(2,1)}), bf16[1,256,8,128]{3,2,0,1:T(8,128)(2,1)S(1)}, u32[]{:S(2)}, u32[]{:S(2)}) async-start(bf16[1,256,8,128]{3,2,0,1:T(8,128)(2,1)} %bitcast.15), calls=%async_computation | async-start | bytes 1048576 | tf_op jit(solution)/shard_map/all_to_all | solution.py:48
  43.3 23.8 %all-to-all-start.1 = ((bf16[1,256,8,128]{3,2,0,1:T(8,128)(2,1)}), bf16[1,256,8,128]{3,2,0,1:T(8,128)(2,1)S(1)}, u32[]{:S(2)}, u32[]{:S(2)}) async-start(bf16[1,256,8,128]{3,2,0,1:T(8,128)(2,1)} %bitcast.19), calls=%async_computation.1 | async-start | bytes 1048576 | tf_op jit(solution)/shard_map/all_to_all | solution.py:49
  67.0 35.9 %all-to-all-start.3 = ((bf16[1,256,8,128]{3,2,0,1:T(8,128)(2,1)}), bf16[1,256,8,128]{3,2,0,1:T(8,128)(2,1)S(1)}, u32[]{:S(2)}, u32[]{:S(2)}) async-start(bf16[1,256,8,128]{3,2,0,1:T(8,128)(2,1)} %bitcast.27), calls=%async_computation.3 | async-start | bytes 1048576 | tf_op jit(solution)/shard_map/all_to_all | solution.py:50
  103.0 21.0 %all-to-all-start.2 = ((bf16[1,256,8,128]{3,2,0,1:T(8,128)(2,1)}), bf16[1,256,8,128]{3,2,0,1:T(8,128)(2,1)S(1)}, u32[]{:S(2)}, u32[]{:S(2)}) async-start(bf16[1,256,8,128]{3,2,0,1:T(8,128)(2,1)} %bitcast.23), calls=%async_computation.2 | async-start | bytes 1048576 | tf_op jit(solution)/shard_map/all_to_all | solution.py:51
  110.4 14.2 %copy-start.2 = (f32[4,8,64,64]{2,3,1,0:T(8,128)}, f32[4,8,64,64]{2,3,1,0:T(8,128)S(1)}, u32[]{:S(2)}) copy-start(f32[4,8,64,64]{2,3,1,0:T(8,128)S(1)} %get-tuple-element.6) | copy-start | bytes 1572868
  128.2 26.1 %all-to-all-start.5 = ((bf16[64,4,8,128]{3,2,1,0:T(8,128)(2,1)}), bf16[64,4,8,128]{3,2,1,0:T(8,128)(2,1)S(1)}, u32[]{:S(2)}, u32[]{:S(2)}) async-start(bf16[64,4,8,128]{3,2,1,0:T(8,128)(2,1)} %copy.38), calls=%async_computation.5 | async-start | bytes 1048576 | tf_op jit(solution)/shard_map/all_to_all | solution.py:56
  154.3 31.5 %all-to-all-start.4 = ((bf16[64,4,8,128]{3,2,1,0:T(8,128)(2,1)}), bf16[64,4,8,128]{3,2,1,0:T(8,128)(2,1)S(1)}, u32[]{:S(2)}, u32[]{:S(2)}) async-start(bf16[64,4,8,128]{3,2,1,0:T(8,128)(2,1)} %copy.36), calls=%async_computation.4 | async-start | bytes 1048576 | tf_op jit(solution)/shard_map/all_to_all | solution.py:55
  185.7 26.7 %all-to-all-start.6 = ((bf16[64,4,8,128]{3,2,1,0:T(8,128)(2,1)}), bf16[64,4,8,128]{3,2,1,0:T(8,128)(2,1)S(1)}, u32[]{:S(2)}, u32[]{:S(2)}) async-start(bf16[64,4,8,128]{3,2,1,0:T(8,128)(2,1)} %copy.40), calls=%async_computation.6 | async-start | bytes 1048576 | tf_op jit(solution)/shard_map/all_to_all | solution.py:57
  192.3 171.5 %reduce-scatter.2.cloned.1.call-start = ((), (), s32[]{:S(2)}) async-start(), calls=%async_computation.9 | async-start | bytes 5242880 | tf_op jit(solution)/shard_map/reduce_scatter | solution.py:72
Sparse Core Ops, SparseCore 0:
  10.7 226.5 all-gather.1
  251.2 112.5 reduce-scatter.1
where the time goes:
time: 374 us; the launch traced here: 373 us
  waiting for transfers between devices  268 us (72%)
  starting transfers between devices  60.2 us (16%)
  matrix products  19.4 us (5%)
  between operations  13.6 us (4%)
  local copies, waits for them, and re-layouts  10.8 us (3%)
    reduce_scatter x1, waiting for transfers between devices, per_device(): lax.psum_scatter(partial_sum, 'head', scatter_dimension=0, tiled=True)  113 us
    all_to_all x1, waiting for transfers between devices, per_device(): lax.all_to_all(sv, 'tm', split_axis=1, concat_axis=0, tiled=True)  30.1 us
    all_gather x1, waiting for transfers between devices, per_device(): lax.all_gather(weights, 'tm', axis=1, tiled=True)  24.6 us
    all_to_all x1, waiting for transfers between devices, per_device(): lax.all_to_all(grads[2], 'tm', split_axis=0, concat_axis=1, tiled=True)  19.5 us
    all_to_all x1, waiting for transfers between devices, per_device(): lax.all_to_all(grads[1], 'tm', split_axis=0, concat_axis=1, tiled=True)  18.6 us
    all_to_all x1, waiting for transfers between devices, per_device(): lax.all_to_all(grads[0], 'tm', split_axis=0, concat_axis=1, tiled=True)  17.4 us
    all_to_all x1, waiting for transfers between devices, per_device(): lax.all_to_all(sq, 'tm', split_axis=1, concat_axis=0, tiled=True)  17 us
    all_to_all x1, starting transfers between devices, per_device(): lax.all_to_all(sq, 'tm', split_axis=1, concat_axis=0, tiled=True)  15.1 us
  transfers between devices with their start and end apart: 9, of which 9 were waited for; matrix products, arithmetic and copies ran while one was open for 4% of the time, Pallas kernels for 0%

commit v1 on v0

v1 whole, which is shorter than its diff:
```python
import jax
import jax.numpy as jnp
import numpy as np
from jax import lax
from jax.experimental import pallas as pl
from jax.experimental.pallas import tpu as pltpu
from jax.sharding import Mesh, PartitionSpec as P

HD = 128
AXES = ("z", "yh", "yl", "xh", "xl", "zl", "c")
TM = AXES[:5]
HEAD = AXES[5:]
BF16 = jnp.bfloat16
F32 = jnp.float32
BY_MESH = pl.DeviceIdType.MESH
ANY = pl.BlockSpec(memory_space=pl.ANY)


def position():
    at = lax.axis_index
    return at("z"), 2 * at("yh") + at("yl"), 2 * at("xh") + at("xl")


def device(z, y, x):
    return {"z": z, "yh": y // 2, "yl": y % 2, "xh": x // 2, "xl": x % 2}


def partner(at, shift):
    return (at + 1 + 2 * ((at + shift) % 2)) % 4


def swap_kernel(src, dst, send_sem, recv_sem, own_sem):
    z, y, x = position()
    me = z * 16 + y * 4 + x
    own = pltpu.make_async_copy(src.at[me], dst.at[me], own_sem)
    own.start()
    barrier = pltpu.get_barrier_semaphore()

    def peer(step):
        return (z + step // 16) % 4, (y + (step // 4) % 4) % 4, (x + step % 4) % 4

    def greet(step, carry):
        pl.semaphore_signal(barrier, inc=1, device_id=device(*peer(step)), device_id_type=BY_MESH)
        return carry

    lax.fori_loop(1, 64, greet, 0)
    pl.semaphore_wait(barrier, 63)

    def send(step, carry):
        pz, py, px = peer(step)
        pltpu.make_async_remote_copy(
            src_ref=src.at[pz * 16 + py * 4 + px],
            dst_ref=dst.at[me],
            send_sem=send_sem,
            recv_sem=recv_sem,
            device_id=device(pz, py, px),
            device_id_type=BY_MESH,
        ).start()
        return carry

    lax.fori_loop(1, 64, send, 0)
    most = pl.ds(0, 63)
    pltpu.make_async_copy(src.at[most], src.at[most], send_sem).wait()
    pltpu.make_async_copy(dst.at[most], dst.at[most], recv_sem).wait()
    own.wait()


def swap(array, collective_id):
    return pl.pallas_call(
        swap_kernel,
        out_shape=jax.ShapeDtypeStruct(array.shape, array.dtype),
        in_specs=[ANY],
        out_specs=ANY,
        scratch_shapes=[pltpu.SemaphoreType.DMA] * 3,
        compiler_params=pltpu.CompilerParams(collective_id=collective_id, has_side_effects=True),
        name=f"swap_{collective_id}",
    )(array)


def share_kernel(src, dst, send_sem, recv_sem, own_sem):
    z, y, x = position()
    slot = (y % 2) * 2 + x % 2
    own = pltpu.make_async_copy(src, dst.at[:, slot], own_sem)
    own.start()
    barrier = pltpu.get_barrier_semaphore()
    for dy, dx in ((0, 1), (0, 3), (1, 0), (3, 0), (1, 1), (1, 3), (3, 1), (3, 3)):
        pl.semaphore_signal(
            barrier, inc=1, device_id=device(z, (y + dy) % 4, (x + dx) % 4), device_id_type=BY_MESH
        )
    pl.semaphore_wait(barrier, 8)
    copies = []
    for role in (2, 0, 1):
        for c in range(4):
            py, px = partner(y, c // 2), partner(x, c % 2)
            target = (device(z, y, px), device(z, py, x), device(z, py, px))[role]
            copy = pltpu.make_async_remote_copy(
                src_ref=src.at[:, c],
                dst_ref=dst.at[:, slot, c],
                send_sem=send_sem.at[role, c],
                recv_sem=recv_sem.at[role, c],
                device_id=target,
                device_id_type=BY_MESH,
            )
            copy.start()
            copies.append(copy)
    for copy in copies:
        copy.wait()
    own.wait()


def share(grads):
    m, c, f, k = grads.shape
    return pl.pallas_call(
        share_kernel,
        out_shape=jax.ShapeDtypeStruct((m, 4, c, f, k), grads.dtype),
        in_specs=[ANY],
        out_specs=ANY,
        scratch_shapes=[
            pltpu.SemaphoreType.DMA((3, 4)),
            pltpu.SemaphoreType.DMA((3, 4)),
            pltpu.SemaphoreType.DMA,
        ],
        compiler_params=pltpu.CompilerParams(collective_id=3, has_side_effects=True),
        name="share",
    )(grads)


def patch_order():
    place = np.zeros((4, 256, 256), np.float32)
    for yl in range(2):
        for xl in range(2):
            row = 0
            for z in range(4):
                for yh in range(2):
                    for xh in range(2):
                        y, x = 2 * yh + yl, 2 * xh + xl
                        for slot in range(4):
                            for c in range(4):
                                ys = y if slot // 2 == yl else partner(y, c // 2)
                                xs = x if slot % 2 == xl else partner(x, c % 2)
                                place[yl * 2 + xl, row, 4 * (z * 16 + ys * 4 + xs) + c] = 1
                                row += 1
    return place


def temporal(q_heads, k_heads, v_heads, g_heads):
    scale = 1.0 / q_heads.shape[-1] ** 0.5
    scores = (
        jnp.einsum("fphd,gphd->phfg", q_heads, k_heads, preferred_element_type=F32) * scale
    )
    probs = jax.nn.softmax(scores, axis=-1)
    probs_b = probs.astype(BF16)
    attended = jnp.einsum("phfg,gphd->fphd", probs_b, v_heads, preferred_element_type=F32)
    delta = jnp.transpose(jnp.sum(g_heads.astype(F32) * attended, axis=-1), (1, 2, 0))
    grad_probs = jnp.einsum("fphd,gphd->phfg", g_heads, v_heads, preferred_element_type=F32)
    grad_scores = (probs * (grad_probs - delta[..., None])).astype(BF16)
    grad_value = jnp.einsum("phfg,fphd->pghd", probs_b, g_heads, preferred_element_type=F32)
    grad_query = (
        jnp.einsum("phfg,gphd->pfhd", grad_scores, k_heads, preferred_element_type=F32) * scale
    )
    grad_key = (
        jnp.einsum("phfg,fphd->pghd", grad_scores, q_heads, preferred_element_type=F32) * scale
    )
    return grad_query.astype(BF16), grad_key.astype(BF16), grad_value.astype(BF16)


def per_device(query, key_in, value, grad_out, weights):
    rows = lax.all_gather(weights, ("z", "yh", "xh"), axis=1, tiled=True)
    packed = jnp.stack([a.reshape(64, 4, 1024) for a in (query, key_in, value, grad_out)], axis=1)
    moved = swap(packed.reshape(64, 16, 1024), 1).reshape(64, 4, 4, 8, HD)
    grads = temporal(moved[:, 0], moved[:, 1], moved[:, 2], moved[:, 3])
    stacked = jnp.stack([a.reshape(4, 64, 1024) for a in grads])
    shared = share(stacked).reshape(3, 1024, 1024)
    partial_sum = jnp.einsum(
        "mtk,mzik->zti", shared, rows.reshape(3, 4, 256, 1024), preferred_element_type=F32
    ).astype(BF16)
    mine = lax.psum_scatter(partial_sum, HEAD, scatter_dimension=0, tiled=True)
    by_frame = jnp.transpose(mine.reshape(16, 64, 256), (1, 0, 2))
    back = swap(by_frame, 2).reshape(4, 2, 2, 2, 2, 16, 2, 2, 64)
    place = jnp.asarray(patch_order(), BF16).reshape(2, 2, 4, 2, 2, 16, 256)
    out = jnp.einsum("zybxatvuk,bazyxtp->vbuakp", back, place, preferred_element_type=F32)
    return out.reshape(1024, 256).astype(BF16)


def solution(mesh):
    fine = Mesh(mesh.devices.reshape(4, 2, 2, 2, 2, 2, 2), AXES)
    placed = (P(TM, HEAD),) * 4 + (P(None, TM, HEAD),)
    return jax.shard_map(
        per_device, mesh=fine, in_specs=placed, out_specs=P(HEAD, TM), check_vma=False
    )
```

time: 374 us -> 271 us (0.72)
  waiting for transfers between devices: 268 us -> 48.6 us
  Pallas kernels: 0 us -> 169 us
  starting transfers between devices: 60.2 us -> 0.04 us
  local copies, waits for them, and re-layouts: 10.8 us -> 16.4 us
    pallas_call x0 -> x3, Pallas kernels: none -> 169 us  [the longest x2 98.9 us: swap(): pl.pallas_call(swap_kernel, out_shape=jax.ShapeDtypeStruct(array.shape, a...]
    all_to_all x7 -> x0, waiting for transfers between devices: 130 us -> none  [the longest x1 30.1 us: per_device(): lax.all_to_all(sv, 'tm', split_axis=1, concat_axis=0, tiled=True)]
    reduce_scatter x1, waiting for transfers between devices: 113 us -> 27.4 us  [per_device(): mine = lax.psum_scatter(partial_sum, HEAD, scatter_dimension=0, tiled=True)]
    all_to_all x7 -> x0, starting transfers between devices: 60 us -> none  [the longest x1 15.1 us: per_device(): lax.all_to_all(sq, 'tm', split_axis=1, concat_axis=0, tiled=True)]
    reshape x0 -> x3, local copies, waits for them, and re-layouts: none -> 6.72 us  [the longest x1 2.51 us: per_device(): back = swap(by_frame, 2).reshape(4, 2, 2, 2, 2, 16, 2, 2, 64)]
    another operation x3 -> x7, local copies, waits for them, and re-layouts: 0.67 us -> 5.13 us  [the longest x4 4.45 us: per_device(): jnp.stack([a.reshape(64, 4, 1024) for a in (query, key_in, value, grad_ou...]
    all_gather x1, waiting for transfers between devices: 24.6 us -> 20.5 us  [per_device(): rows = lax.all_gather(weights, ('z', 'yh', 'xh'), axis=1, tiled=True)]
    another operation x0 -> x2, other arithmetic: none -> 4 us  [the longest x1 2.63 us: per_device(): jnp.stack([a.reshape(64, 4, 1024) for a in (query, key_in, value, grad_ou...]
  transfers between devices with their start and end apart: 9 -> 2, of which waited for: 9 -> 2; matrix products, arithmetic and copies ran while one was open for 4% -> 8% of each run, Pallas kernels for 0% -> 53%
where the time goes in v1:
time: 271 us; the launch traced here: 270 us
  Pallas kernels  169 us (62%)
  waiting for transfers between devices  48.6 us (18%)
  matrix products  18.5 us (7%)
  local copies, waits for them, and re-layouts  16.4 us (6%)
  between operations  13.6 us (5%)
  other arithmetic  4 us (1%)
    pallas_call x2, Pallas kernels, swap(): pl.pallas_call(swap_kernel, out_shape=jax.ShapeDtypeStruct(array.shape, a...  98.9 us
    pallas_call x1, Pallas kernels, share(): pl.pallas_call(share_kernel, out_shape=jax.ShapeDtypeStruct((m, 4, c, f,...  70.3 us
    reduce_scatter x1, waiting for transfers between devices, per_device(): mine = lax.psum_scatter(partial_sum, HEAD, scatter_dimension=0, tiled=True)  27.4 us
    all_gather x1, waiting for transfers between devices, per_device(): rows = lax.all_gather(weights, ('z', 'yh', 'xh'), axis=1, tiled=True)  20.5 us
    dot_general x1, matrix products, per_device(): jnp.einsum('mtk,mzik->zti', shared, rows.reshape(3, 4, 256, 1024), prefer...  11.6 us
  transfers between devices with their start and end apart: 2, of which 2 were waited for; matrix products, arithmetic and copies ran while one was open for 8% of the time, Pallas kernels for 53%

profile of v1, /device:TPU:1, one launch (start us, length us, event | category | flops | bytes accessed | tf_op | source)
XLA Modules:
  0.0 270.4 jit_solution(10196903216801064000)
XLA Ops:
  6.5 0.7 all-gather.2.cloned.1.call-update
  7.3 1.2 stack_reshape.21
  8.5 1.2 stack_reshape.22
  9.8 1.0 stack_reshape.23
  10.8 1.0 stack_reshape.24
  11.8 2.6 pad_maximum_fusion
  14.4 2.1 reshape.26.src
  16.5 72.9 %swap_1.1 = bf16[64,16,1024]{2,1,0:T(8,128)(2,1)} custom-call(bf16[64,16,1024]{2,1,0:T(8,128)(2,1)} %reshape.26.src), custom_call_target="tpu_custom_call" | custom-call | tf_op jit(solution)/shard_map/swap_1/pallas_call | solution.py:69
  89.4 2.2 copy.50
  91.6 0.4 fusion.21
  92.0 1.6 fusion.22
  93.6 1.6 fusion.14
  95.2 0.3 copy.35
  95.6 0.2 stack_reshape.27
  95.8 1.9 fusion.10
  97.8 0.6 fusion.6
  98.3 0.4 fusion.12
  98.7 0.3 copy.33
  99.1 0.2 stack_reshape.25
  99.3 0.3 fusion.11
  99.6 0.3 copy.34
  100.0 0.2 stack_reshape.26
  100.2 1.4 pad_maximum_fusion.1.src
  101.6 70.3 %share.1 = bf16[3,4,4,64,1024]{4,3,2,1,0:T(8,128)(2,1)} custom-call(bf16[3,4,64,1024]{3,2,1,0:T(8,128)(2,1)} %pad_maximum_fusion.1.src), custom_call_target="tpu_custom_call" | custom-call | tf_op jit(solution)/shard_map/share/pallas_call | solution.py:113
  171.9 20.5 %all-gather.2.cloned.1.call-done = bf16[3,1024,1024]{2,1,0:T(8,128)(2,1)} async-done(((bf16[3,64,1024]{2,1,0:T(8,128)(2,1)}), bf16[3,1024,1024]{2,1,0:T(8,128)(2,1)}) %all-gather.2.cloned.1.call-update) | async-done | bytes 6291472 | tf_op jit(solution)/shard_map/all_gather | solution.py:168
  192.4 11.6 %fusion.1 = bf16[4,1024,256]{2,1,0:T(8,128)(2,1)} fusion(bf16[3,1024,1024,1]{2,1,3,0:T(8,128)(2,1)} %bitcast.97, bf16[3,4,256,1024]{3,2,1,0:T(8,128)(2,1)} %bitcast.104), kind=kOutput, calls=%fused_computation.3 | convolution fusion | flops 6443499520 | bytes 14680064 | tf_op jit(solution)/shard_map/mtk,mzik->zti/dot_general | solution.py:174
  204.1 27.4 %reduce-scatter.2.cloned.1.call-done = bf16[1,1024,256]{2,1,0:T(8,128)(2,1)} async-done(((bf16[4,1024,256]{2,1,0:T(8,128)(2,1)}), bf16[1,1024,256]{2,1,0:T(8,128)(2,1)}) %reduce-scatter.2.cloned.1.call-update) | async-done | bytes 524304 | tf_op jit(solution)/shard_map/reduce_scatter | solution.py:177
  231.5 2.1 copy.80
  233.6 26.1 %swap_2.1 = bf16[64,16,256]{2,1,0:T(8,128)(2,1)} custom-call(bf16[64,16,256]{2,1,0:T(8,128)(2,1)} %bitcast.98), custom_call_target="tpu_custom_call" | custom-call | tf_op jit(solution)/shard_map/swap_2/pallas_call | solution.py:69
  259.7 2.5 reshape.31
  262.2 0.5 fusion.13
  262.7 0.8 copy.39
  (11 shorter events, 0.1 us)
Async XLA Ops:
  6.5 3.3 %copy-start = (bf16[256,1024]{1,0:T(8,128)(2,1)S(1)}, bf16[256,1024]{1,0:T(8,128)(2,1)}, u32[]{:S(2)}) copy-start(bf16[256,1024]{1,0:T(8,128)(2,1)} %param.8) | copy-start | bytes 1572868
  6.5 4.3 %copy-start.1 = (bf16[256,1024]{1,0:T(8,128)(2,1)S(1)}, bf16[256,1024]{1,0:T(8,128)(2,1)}, u32[]{:S(2)}) copy-start(bf16[256,1024]{1,0:T(8,128)(2,1)} %param.9) | copy-start | bytes 1572868
  6.5 185.9 %all-gather.2.cloned.1.call-start = ((), (), s32[]{:S(2)}) async-start(), calls=%async_computation.1 | async-start | bytes 6684672 | tf_op jit(solution)/shard_map/all_gather | solution.py:168
  7.3 224.2 %reduce-scatter.2.cloned.1.call-start = ((), (), s32[]{:S(2)}) async-start(), calls=%async_computation.2 | async-start | bytes 2621440 | tf_op jit(solution)/shard_map/reduce_scatter | solution.py:177
  95.8 1.9 copy-start.3
  204.1 58.2 %copy-start.2 = (bf16[2,2,4,2,2,16,256,1,1]{6,5,2,3,4,8,7,1,0:T(8,128)(2,1)S(1)}, bf16[2,2,4,2,2,16,256,1,1]{6,5,2,3,4,8,7,1,0:T(8,128)(2,1)}, u32[]{:S(2)}) copy-start(bf16[2,2,4,2,2,16,256,1,1]{6,5,2,3,4,8,7,1,0:T(8,128)(2,1)} %constant.12) | copy-start | bytes 1572868
Sparse Core Ops, SparseCore 0:
  10.9 181.4 all-gather.1
  204.2 27.2 reduce-scatter.1

commit v2 on v1

v2 whole, which is shorter than its diff:
```python
import functools

import jax
import jax.numpy as jnp
import numpy as np
from jax import lax
from jax.experimental import pallas as pl
from jax.experimental.pallas import tpu as pltpu
from jax.sharding import Mesh, PartitionSpec as P

HD = 128
AXES = ("z", "y", "x", "zl", "c")
TM = AXES[:3]
HEAD = AXES[3:]
BF16 = jnp.bfloat16
F32 = jnp.float32
BY_MESH = pl.DeviceIdType.MESH
ANY = pl.BlockSpec(memory_space=pl.ANY)


def position():
    return lax.axis_index("z"), lax.axis_index("y"), lax.axis_index("x")


def swap_kernel(y_major, src, dst, send_sem, recv_sem, own_sem):
    z, y, x = position()
    me = z * 16 + y * 4 + x
    slot = y * 16 + z * 4 + x if y_major else me
    own = pltpu.make_async_copy(src.at[me], dst.at[slot], own_sem)
    own.start()
    barrier = pltpu.get_barrier_semaphore()

    def peer(step):
        return (z + step // 16) % 4, (y + (step // 4) % 4) % 4, (x + step % 4) % 4

    def greet(step, carry):
        pl.semaphore_signal(barrier, inc=1, device_id=dict(zip(TM, peer(step))), device_id_type=BY_MESH)
        return carry

    lax.fori_loop(1, 64, greet, 0)
    pl.semaphore_wait(barrier, 63)

    def send(step, carry):
        pz, py, px = peer(step)
        pltpu.make_async_remote_copy(
            src_ref=src.at[pz * 16 + py * 4 + px],
            dst_ref=dst.at[slot],
            send_sem=send_sem,
            recv_sem=recv_sem,
            device_id={"z": pz, "y": py, "x": px},
            device_id_type=BY_MESH,
        ).start()
        return carry

    lax.fori_loop(1, 64, send, 0)
    most = pl.ds(0, 63)
    pltpu.make_async_copy(src.at[most], src.at[most], send_sem).wait()
    pltpu.make_async_copy(dst.at[most], dst.at[most], recv_sem).wait()
    own.wait()


def swap(array, collective_id, y_major):
    return pl.pallas_call(
        functools.partial(swap_kernel, y_major),
        out_shape=jax.ShapeDtypeStruct(array.shape, array.dtype),
        in_specs=[ANY],
        out_specs=ANY,
        scratch_shapes=[pltpu.SemaphoreType.DMA] * 3,
        compiler_params=pltpu.CompilerParams(collective_id=collective_id, has_side_effects=True),
        name=f"swap_{collective_id}",
    )(array)


def share_kernel(src, dst, send_sem, recv_sem, own_sem):
    y = lax.axis_index("y")
    up, down = (y + 1) % 4, (y + 3) % 4
    own = pltpu.make_async_copy(src, dst.at[:, y], own_sem)
    own.start()
    barrier = pltpu.get_barrier_semaphore()
    for target in (up, down):
        pl.semaphore_signal(barrier, inc=1, device_id={"y": target}, device_id_type=BY_MESH)
    pl.semaphore_wait(barrier, 2)

    def send(block, slot, c, target, lane):
        copy = pltpu.make_async_remote_copy(
            src_ref=block,
            dst_ref=dst.at[:, slot, c],
            send_sem=send_sem.at[lane, c],
            recv_sem=recv_sem.at[lane, c],
            device_id={"y": target},
            device_id_type=BY_MESH,
        )
        copy.start()
        return copy

    ups, downs, far = {}, {}, []
    for step in range(4):
        c, d = step, (step + 2) % 4
        ups[c] = send(src.at[:, c], y, c, up, 0)
        downs[d] = send(src.at[:, d], y, d, down, 1)
    for step in range(2):
        c, d = step, step + 2
        ups[c].wait_recv()
        far.append(send(dst.at[:, down, c], down, c, up, 2))
        downs[d].wait_recv()
        far.append(send(dst.at[:, up, d], up, d, down, 2))
    for step in range(2):
        ups[step + 2].wait_recv()
        downs[step].wait_recv()
    for copy in far:
        copy.wait_recv()
    for copy in (*ups.values(), *downs.values(), *far):
        copy.wait_send()
    own.wait()


def share(grads):
    m, c, f, k = grads.shape
    return pl.pallas_call(
        share_kernel,
        out_shape=jax.ShapeDtypeStruct((m, 4, c, f, k), grads.dtype),
        in_specs=[ANY],
        out_specs=ANY,
        scratch_shapes=[
            pltpu.SemaphoreType.DMA((3, 4)),
            pltpu.SemaphoreType.DMA((3, 4)),
            pltpu.SemaphoreType.DMA,
        ],
        compiler_params=pltpu.CompilerParams(collective_id=3, has_side_effects=True),
        name="share",
    )(grads)


def patch_order():
    z, x, slot, c = np.indices((4, 4, 4, 4)).reshape(4, 256)
    return np.eye(256, dtype=np.float32)[4 * (z * 16 + slot * 4 + x) + c]


def temporal(q_heads, k_heads, v_heads, g_heads):
    scale = 1.0 / q_heads.shape[-1] ** 0.5
    scores = (
        jnp.einsum("fphd,gphd->phfg", q_heads, k_heads, preferred_element_type=F32) * scale
    )
    probs = jax.nn.softmax(scores, axis=-1)
    probs_b = probs.astype(BF16)
    attended = jnp.einsum("phfg,gphd->fphd", probs_b, v_heads, preferred_element_type=F32)
    delta = jnp.transpose(jnp.sum(g_heads.astype(F32) * attended, axis=-1), (1, 2, 0))
    grad_probs = jnp.einsum("fphd,gphd->phfg", g_heads, v_heads, preferred_element_type=F32)
    grad_scores = (probs * (grad_probs - delta[..., None])).astype(BF16)
    grad_value = jnp.einsum("phfg,fphd->pghd", probs_b, g_heads, preferred_element_type=F32)
    grad_query = (
        jnp.einsum("phfg,gphd->pfhd", grad_scores, k_heads, preferred_element_type=F32) * scale
    )
    grad_key = (
        jnp.einsum("phfg,fphd->pghd", grad_scores, q_heads, preferred_element_type=F32) * scale
    )
    return grad_query.astype(BF16), grad_key.astype(BF16), grad_value.astype(BF16)


def per_device(query, key_in, value, grad_out, weights):
    rows = lax.all_gather(weights, ("z", "x"), axis=1, tiled=True)
    packed = jnp.stack([a.reshape(64, 4, 1024) for a in (query, key_in, value, grad_out)], axis=1)
    moved = swap(packed.reshape(64, 16, 1024), 1, False).reshape(64, 4, 4, 8, HD)
    grads = temporal(moved[:, 0], moved[:, 1], moved[:, 2], moved[:, 3])
    stacked = jnp.stack([a.reshape(4, 64, 1024) for a in grads])
    shared = share(stacked).reshape(3, 1024, 1024)
    partial_sum = jnp.einsum(
        "mtk,mzik->zti", shared, rows.reshape(3, 4, 256, 1024), preferred_element_type=F32
    ).astype(BF16)
    mine = lax.psum_scatter(partial_sum, HEAD, scatter_dimension=0, tiled=True)
    by_frame = jnp.transpose(mine.reshape(16, 64, 256), (1, 0, 2))
    back = swap(by_frame, 2, True).reshape(4, 256, 256)
    place = jnp.asarray(patch_order(), BF16)
    out = jnp.einsum("ytk,tp->ykp", back, place, preferred_element_type=F32)
    return out.reshape(1024, 256).astype(BF16)


def solution(mesh):
    fine = Mesh(mesh.devices.reshape(4, 4, 4, 2, 2), AXES)
    placed = (P(TM, HEAD),) * 4 + (P(None, TM, HEAD),)
    return jax.shard_map(
        per_device, mesh=fine, in_specs=placed, out_specs=P(HEAD, TM), check_vma=False
    )
```

time: 271 us -> 237 us (0.87)
  waiting for transfers between devices: 48.6 us -> 31.9 us
  Pallas kernels: 169 us -> 153 us
    all_gather x1, waiting for transfers between devices: 20.5 us -> 0.02 us  [per_device(): rows = lax.all_gather(weights, ('z', 'x'), axis=1, tiled=True)]
    pallas_call x1, Pallas kernels: 70.3 us -> 57.3 us  [share(): pl.pallas_call(share_kernel, out_shape=jax.ShapeDtypeStruct((m, 4, c, f,...]
    reduce_scatter x1, waiting for transfers between devices: 27.4 us -> 31.2 us  [per_device(): mine = lax.psum_scatter(partial_sum, HEAD, scatter_dimension=0, tiled=True)]
    pallas_call x2, Pallas kernels: 98.9 us -> 95.7 us  [swap(): pl.pallas_call(functools.partial(swap_kernel, y_major), out_shape=jax.Sha...]
  transfers between devices with their start and end apart: 2 -> 2, of which waited for: 2 -> 1; matrix products, arithmetic and copies ran while one was open for 8% -> 9% of each run, Pallas kernels for 53% -> 54%
where the time goes in v2:
time: 237 us; the launch traced here: 236 us
  Pallas kernels  153 us (65%)
  waiting for transfers between devices  31.9 us (13%)
  matrix products  19.4 us (8%)
  local copies, waits for them, and re-layouts  14.3 us (6%)
  between operations  13.6 us (6%)
  other arithmetic  4 us (2%)
    pallas_call x2, Pallas kernels, swap(): pl.pallas_call(functools.partial(swap_kernel, y_major), out_shape=jax.Sha...  95.7 us
    pallas_call x1, Pallas kernels, share(): pl.pallas_call(share_kernel, out_shape=jax.ShapeDtypeStruct((m, 4, c, f,...  57.3 us
    reduce_scatter x1, waiting for transfers between devices, per_device(): mine = lax.psum_scatter(partial_sum, HEAD, scatter_dimension=0, tiled=True)  31.2 us
    dot_general x1, matrix products, per_device(): jnp.einsum('mtk,mzik->zti', shared, rows.reshape(3, 4, 256, 1024), prefer...  11.6 us
  transfers between devices with their start and end apart: 2, of which 1 were waited for; matrix products, arithmetic and copies ran while one was open for 9% of the time, Pallas kernels for 54%

profile of v2, /device:TPU:1, one launch (start us, length us, event | category | flops | bytes accessed | tf_op | source)
XLA Modules:
  0.0 236.3 jit_solution(11927706172869886683)
XLA Ops:
  6.5 0.7 all-gather.2.cloned.1.call-update
  7.3 0.0 reduce-scatter.2.cloned.1.call-start
  7.3 1.2 stack_reshape.21
  8.5 1.2 stack_reshape.22
  9.8 1.0 stack_reshape.23
  10.8 1.0 stack_reshape.24
  11.8 2.6 %pad_maximum_fusion = bf16[64,4,4,1024]{3,2,1,0:T(4,128)(2,1)S(1)} fusion(bf16[64,1,4,1024]{3,2,1,0:T(4,128)(2,1)} %bitcast.95, bf16[64,1,4,1024]{3,2,1,0:T(4,128)(2,1)} %bitcast.94, bf16[64,1,4,1024]{3,2,1,0:T(4,128)(2,1)S(1)} %bitcast.93, bf16[64,1,4,1024]{3,2,1,0:T(4,128)(2,1)S(1)} %bitcast.92), kind=kLoop, calls=%fused_computation.2 | loop fusion | flops 3145728 | bytes 4194304 | tf_op jit(solution)/shard_map/stack | solution.py:162
  14.4 2.1 reshape.23.src
  16.5 71.0 %swap_1.1 = bf16[64,16,1024]{2,1,0:T(8,128)(2,1)} custom-call(bf16[64,16,1024]{2,1,0:T(8,128)(2,1)} %reshape.23.src), custom_call_target="tpu_custom_call" | custom-call | tf_op jit(solution)/shard_map/swap_1/pallas_call | solution.py:63
  87.5 2.2 copy.46
  89.7 0.4 fusion.18
  90.1 1.6 fusion.19
  91.8 1.9 fusion.12
  93.7 0.3 copy.34
  94.0 0.2 stack_reshape.27
  94.3 1.9 fusion.9
  96.2 0.6 fusion.6
  96.8 0.4 fusion.11
  97.2 0.3 copy.32
  97.5 0.2 stack_reshape.25
  97.7 0.3 fusion.10
  98.1 0.3 copy.33
  98.4 0.2 stack_reshape.26
  98.7 1.4 pad_maximum_fusion.1.src
  100.0 57.3 %share.1 = bf16[3,4,4,64,1024]{4,3,2,1,0:T(8,128)(2,1)} custom-call(bf16[3,4,64,1024]{3,2,1,0:T(8,128)(2,1)} %pad_maximum_fusion.1.src), custom_call_target="tpu_custom_call" | custom-call | tf_op jit(solution)/shard_map/share/pallas_call | solution.py:119
  157.3 0.0 all-gather.2.cloned.1.call-done
  157.4 11.6 %fusion.1 = bf16[4,1024,256]{2,1,0:T(8,128)(2,1)} fusion(bf16[3,1024,1024,1]{2,1,3,0:T(8,128)(2,1)} %bitcast.88, bf16[3,4,256,1024]{3,2,1,0:T(8,128)(2,1)} %bitcast.97), kind=kOutput, calls=%fused_computation.3 | convolution fusion | flops 6443499520 | bytes 14680064 | tf_op jit(solution)/shard_map/mtk,mzik->zti/dot_general | solution.py:167
  169.0 31.2 %reduce-scatter.2.cloned.1.call-done = bf16[1,1024,256]{2,1,0:T(8,128)(2,1)} async-done(((bf16[4,1024,256]{2,1,0:T(8,128)(2,1)}), bf16[1,1024,256]{2,1,0:T(8,128)(2,1)}) %reduce-scatter.2.cloned.1.call-update) | async-done | bytes 524304 | tf_op jit(solution)/shard_map/reduce_scatter | solution.py:170
  200.2 2.1 copy.74
  202.3 24.7 %swap_2.1 = bf16[64,16,256]{2,1,0:T(8,128)(2,1)} custom-call(bf16[64,16,256]{2,1,0:T(8,128)(2,1)} %bitcast.90), custom_call_target="tpu_custom_call" | custom-call | tf_op jit(solution)/shard_map/swap_2/pallas_call | solution.py:63
  227.1 1.2 copy.37
  228.4 1.1 convolution_convert_fusion.1
  (10 shorter events, 0.0 us)
Async XLA Ops:
  6.5 3.3 %copy-start = (bf16[256,1024]{1,0:T(8,128)(2,1)S(1)}, bf16[256,1024]{1,0:T(8,128)(2,1)}, u32[]{:S(2)}) copy-start(bf16[256,1024]{1,0:T(8,128)(2,1)} %param.8) | copy-start | bytes 1572868
  6.5 4.3 %copy-start.1 = (bf16[256,1024]{1,0:T(8,128)(2,1)S(1)}, bf16[256,1024]{1,0:T(8,128)(2,1)}, u32[]{:S(2)}) copy-start(bf16[256,1024]{1,0:T(8,128)(2,1)} %param.9) | copy-start | bytes 1572868
  6.5 150.8 %all-gather.2.cloned.1.call-start = ((), (), s32[]{:S(2)}) async-start(), calls=%async_computation.1 | async-start | bytes 6684672 | tf_op jit(solution)/shard_map/all_gather | solution.py:161
  7.3 193.0 %reduce-scatter.2.cloned.1.call-start = ((), (), s32[]{:S(2)}) async-start(), calls=%async_computation.2 | async-start | bytes 2621440 | tf_op jit(solution)/shard_map/reduce_scatter | solution.py:170
  94.2 1.9 copy-start.3
  169.0 59.3 %copy-start.2 = (bf16[256,256]{1,0:T(8,128)(2,1)S(1)}, bf16[256,256]{1,0:T(8,128)(2,1)}, u32[]{:S(2)}) copy-start(bf16[256,256]{1,0:T(8,128)(2,1)} %constant.2.clone) | copy-start | bytes 393220
Sparse Core Ops, SparseCore 0:
  9.8 131.4 all-gather.1
  169.2 31.0 reduce-scatter.1

commit v3 on v2

--- a/solution.py
+++ b/solution.py
@@ -1,5 +1,3 @@
-import functools
-
 import jax
 import jax.numpy as jnp
 import numpy as np
@@ -22,11 +20,10 @@
     return lax.axis_index("z"), lax.axis_index("y"), lax.axis_index("x")
 
 
-def swap_kernel(y_major, src, dst, send_sem, recv_sem, own_sem):
+def swap_kernel(src, dst, send_sem, recv_sem, own_sem):
     z, y, x = position()
     me = z * 16 + y * 4 + x
-    slot = y * 16 + z * 4 + x if y_major else me
-    own = pltpu.make_async_copy(src.at[me], dst.at[slot], own_sem)
+    own = pltpu.make_async_copy(src.at[me], dst.at[me], own_sem)
     own.start()
     barrier = pltpu.get_barrier_semaphore()
 
@@ -44,7 +41,7 @@
         pz, py, px = peer(step)
         pltpu.make_async_remote_copy(
             src_ref=src.at[pz * 16 + py * 4 + px],
-            dst_ref=dst.at[slot],
+            dst_ref=dst.at[me],
             send_sem=send_sem,
             recv_sem=recv_sem,
             device_id={"z": pz, "y": py, "x": px},
@@ -59,9 +56,9 @@
     own.wait()
 
 
-def swap(array, collective_id, y_major):
+def swap(array, collective_id):
     return pl.pallas_call(
-        functools.partial(swap_kernel, y_major),
+        swap_kernel,
         out_shape=jax.ShapeDtypeStruct(array.shape, array.dtype),
         in_specs=[ANY],
         out_specs=ANY,
@@ -131,8 +128,98 @@
     )(grads)
 
 
+def deliver_kernel(part, dst, other, total, core_send, core_recv, send_sem, recv_sem, own_sem):
+    z, y, x = position()
+    zl, core = lax.axis_index("zl"), lax.axis_index("c")
+    slot = ((y * 4 + z) * 4 + x) * 2 + zl
+    barrier = pltpu.get_barrier_semaphore()
+
+    def peer(step):
+        return {
+            "z": (z + step // 16) % 4,
+            "y": (y + (step // 4) % 4) % 4,
+            "x": (x + step % 4) % 4,
+        }
+
+    def greet(first, half):
+        def body(step, carry):
+            pl.semaphore_signal(
+                barrier, inc=1, device_id={**peer(step), "zl": half}, device_id_type=BY_MESH
+            )
+            return carry
+
+        lax.fori_loop(first, 64, body, 0)
+
+    pl.semaphore_signal(barrier, inc=1, device_id={"c": 1 - core}, device_id_type=BY_MESH)
+    greet(0, 1 - zl)
+    greet(1, zl)
+    pl.semaphore_wait(barrier, 128)
+
+    halves = (1 - zl, zl)
+    copies = []
+    for at, half in enumerate(halves):
+        copy = pltpu.make_async_remote_copy(
+            src_ref=part.at[2 * half + 1 - core],
+            dst_ref=other.at[at],
+            send_sem=core_send.at[at],
+            recv_sem=core_recv.at[at],
+            device_id={"c": 1 - core},
+            device_id_type=BY_MESH,
+        )
+        copy.start()
+        copies.append(copy)
+    for at, half in enumerate(halves):
+        copies[at].wait_recv()
+        both = part[2 * half + core].astype(F32) + other[at].astype(F32)
+        total[at] = pltpu.einshape("abk->bak", both.reshape(16, 64, 256)).astype(BF16)
+
+        def send(step, carry):
+            to = peer(step)
+            pltpu.make_async_remote_copy(
+                src_ref=total.at[at, to["z"] * 16 + to["y"] * 4 + to["x"]],
+                dst_ref=dst.at[slot],
+                send_sem=send_sem,
+                recv_sem=recv_sem,
+                device_id={**to, "zl": half},
+                device_id_type=BY_MESH,
+            ).start()
+            return carry
+
+        lax.fori_loop(at, 64, send, 0)
+    own = pltpu.make_async_copy(total.at[1, z * 16 + y * 4 + x], dst.at[slot], own_sem)
+    own.start()
+    most = dst.at[pl.ds(0, 127)]
+    pltpu.make_async_copy(most, most, send_sem).wait()
+    pltpu.make_async_copy(most, most, recv_sem).wait()
+    for copy in copies:
+        copy.wait_send()
+    own.wait()
+
+
+def deliver(part):
+    return pl.pallas_call(
+        deliver_kernel,
+        out_shape=jax.ShapeDtypeStruct((128, 16, 256), part.dtype),
+        in_specs=[pl.BlockSpec(memory_space=pltpu.VMEM)],
+        out_specs=ANY,
+        scratch_shapes=[
+            pltpu.VMEM((2, 1024, 256), part.dtype),
+            pltpu.VMEM((2, 64, 16, 256), part.dtype),
+            pltpu.SemaphoreType.DMA((2,)),
+            pltpu.SemaphoreType.DMA((2,)),
+            pltpu.SemaphoreType.DMA,
+            pltpu.SemaphoreType.DMA,
+            pltpu.SemaphoreType.DMA,
+        ],
+        compiler_params=pltpu.CompilerParams(
+            collective_id=2, has_side_effects=True, vmem_limit_bytes=24 << 20
+        ),
+        name="deliver",
+    )(part)
+
+
 def patch_order():
-    z, x, slot, c = np.indices((4, 4, 4, 4)).reshape(4, 256)
+    z, x, _, slot, c = np.indices((4, 4, 2, 4, 4)).reshape(5, 512)
     return np.eye(256, dtype=np.float32)[4 * (z * 16 + slot * 4 + x) + c]
 
 
@@ -160,16 +247,14 @@
 def per_device(query, key_in, value, grad_out, weights):
     rows = lax.all_gather(weights, ("z", "x"), axis=1, tiled=True)
     packed = jnp.stack([a.reshape(64, 4, 1024) for a in (query, key_in, value, grad_out)], axis=1)
-    moved = swap(packed.reshape(64, 16, 1024), 1, False).reshape(64, 4, 4, 8, HD)
+    moved = swap(packed.reshape(64, 16, 1024), 1).reshape(64, 4, 4, 8, HD)
     grads = temporal(moved[:, 0], moved[:, 1], moved[:, 2], moved[:, 3])
     stacked = jnp.stack([a.reshape(4, 64, 1024) for a in grads])
     shared = share(stacked).reshape(3, 1024, 1024)
     partial_sum = jnp.einsum(
         "mtk,mzik->zti", shared, rows.reshape(3, 4, 256, 1024), preferred_element_type=F32
     ).astype(BF16)
-    mine = lax.psum_scatter(partial_sum, HEAD, scatter_dimension=0, tiled=True)
-    by_frame = jnp.transpose(mine.reshape(16, 64, 256), (1, 0, 2))
-    back = swap(by_frame, 2, True).reshape(4, 256, 256)
+    back = deliver(partial_sum).reshape(4, 512, 256)
     place = jnp.asarray(patch_order(), BF16)
     out = jnp.einsum("ytk,tp->ykp", back, place, preferred_element_type=F32)
     return out.reshape(1024, 256).astype(BF16)

time: 237 us -> 218 us (0.920)
  waiting for transfers between devices: 31.9 us -> 0.73 us
  Pallas kernels: 153 us -> 168 us
  local copies, waits for them, and re-layouts: 14.3 us -> 11.4 us
    reduce_scatter x1 -> x0, waiting for transfers between devices: 31.2 us -> none  [per_device(): mine = lax.psum_scatter(partial_sum, HEAD, scatter_dimension=0, tiled=True)]
    pallas_call x2, Pallas kernels: 95.7 us -> 110 us  [the longest x1 71.1 us: swap(): pl.pallas_call(swap_kernel, out_shape=jax.ShapeDtypeStruct(array.shape, a...]
    reshape x3 -> x2, local copies, waits for them, and re-layouts: 5.45 us -> 2.63 us  [the longest x1 2.09 us: per_device(): moved = swap(packed.reshape(64, 16, 1024), 1).reshape(64, 4, 4, 8, HD)]
  transfers between devices with their start and end apart: 2 -> 1, of which waited for: 1 -> 0; matrix products, arithmetic and copies ran while one was open for 9% -> 10% of each run, Pallas kernels for 54% -> 60%
where the time goes in v3:
time: 218 us; the launch traced here: 216 us
  Pallas kernels  168 us (77%)
  matrix products  18.3 us (8%)
  between operations  13.6 us (6%)
  local copies, waits for them, and re-layouts  11.4 us (5%)
  other arithmetic  4 us (2%)
    pallas_call x1, Pallas kernels, swap(): pl.pallas_call(swap_kernel, out_shape=jax.ShapeDtypeStruct(array.shape, a...  71.1 us
    pallas_call x1, Pallas kernels, share(): pl.pallas_call(share_kernel, out_shape=jax.ShapeDtypeStruct((m, 4, c, f,...  57.5 us
    pallas_call x1, Pallas kernels, deliver(): pl.pallas_call(deliver_kernel, out_shape=jax.ShapeDtypeStruct((128, 16, 2...  39 us
    dot_general x1, matrix products, per_device(): jnp.einsum('mtk,mzik->zti', shared, rows.reshape(3, 4, 256, 1024), prefer...  10.7 us
    another operation x4, local copies, waits for them, and re-layouts, per_device(): jnp.stack([a.reshape(64, 4, 1024) for a in (query, key_in, value, grad_ou...  4.45 us
  transfers between devices with their start and end apart: 1, of which 0 were waited for; matrix products, arithmetic and copies ran while one was open for 10% of the time, Pallas kernels for 60%

profile of v3, /device:TPU:1, one launch (start us, length us, event | category | flops | bytes accessed | tf_op | source)
XLA Modules:
  0.0 215.7 jit_solution(8119627256571664714)
XLA Ops:
  6.5 0.7 all-gather.2.cloned.1.call-update
  7.3 1.2 stack_reshape.21
  8.5 1.2 stack_reshape.22
  9.8 1.0 stack_reshape.23
  10.7 0.0 copy-done.1
  10.7 1.0 stack_reshape.24
  11.7 2.6 %pad_maximum_fusion = bf16[64,4,4,1024]{3,2,1,0:T(4,128)(2,1)S(1)} fusion(bf16[64,1,4,1024]{3,2,1,0:T(4,128)(2,1)} %bitcast.90, bf16[64,1,4,1024]{3,2,1,0:T(4,128)(2,1)} %bitcast.89, bf16[64,1,4,1024]{3,2,1,0:T(4,128)(2,1)S(1)} %bitcast.88, bf16[64,1,4,1024]{3,2,1,0:T(4,128)(2,1)S(1)} %bitcast.87), kind=kLoop, calls=%fused_computation.2 | loop fusion | flops 3145728 | bytes 4194304 | tf_op jit(solution)/shard_map/stack | solution.py:249
  14.4 2.1 reshape.20.src
  16.5 71.1 %swap_1.1 = bf16[64,16,1024]{2,1,0:T(8,128)(2,1)} custom-call(bf16[64,16,1024]{2,1,0:T(8,128)(2,1)} %reshape.20.src), custom_call_target="tpu_custom_call" | custom-call | tf_op jit(solution)/shard_map/swap_1/pallas_call | solution.py:60
  87.6 2.2 %copy.45 = bf16[128,8,8,128]{3,2,1,0:T(8,128)(2,1)S(1)} copy(bf16[128,8,8,128]{3,1,2,0:T(8,128)(2,1)} %bitcast.84) | data formatting | bytes 4194304
  89.8 0.4 fusion.18
  90.2 1.6 fusion.19
  91.8 1.6 fusion.12
  93.4 0.3 copy.34
  93.8 0.2 stack_reshape.27
  94.0 0.0 copy-start.3
  94.0 1.9 fusion.9
  96.0 0.6 fusion.6
  96.5 0.4 fusion.11
  96.9 0.3 copy.32
  97.3 0.2 stack_reshape.25
  97.5 0.3 fusion.10
  97.8 0.3 copy.33
  98.2 0.2 stack_reshape.26
  98.4 1.4 pad_maximum_fusion.1.src
  99.8 57.5 %share.1 = bf16[3,4,4,64,1024]{4,3,2,1,0:T(8,128)(2,1)} custom-call(bf16[3,4,64,1024]{3,2,1,0:T(8,128)(2,1)} %pad_maximum_fusion.1.src), custom_call_target="tpu_custom_call" | custom-call | tf_op jit(solution)/shard_map/share/pallas_call | solution.py:116
  157.3 0.0 all-gather.2.cloned.1.call-done
  157.3 10.7 %fusion.1.part = bf16[4,1024,256]{2,1,0:T(8,128)(2,1)S(1)} fusion(bf16[3,1024,1024,1]{2,1,3,0:T(8,128)(2,1)} %bitcast.85, bf16[3,4,256,1024]{3,2,1,0:T(8,128)(2,1)} %bitcast.91), kind=kOutput, calls=%fused_computation.3 | convolution fusion | flops 6443499520 | bytes 14680064 | tf_op jit(solution)/shard_map/mtk,mzik->zti/dot_general | solution.py:254
  168.0 0.0 copy-start.2
  168.0 39.0 %deliver.1 = bf16[128,16,256]{2,1,0:T(8,128)(2,1)S(1)} custom-call(bf16[4,1024,256]{2,1,0:T(8,128)(2,1)S(1)} %fusion.1.part), custom_call_target="tpu_custom_call" | custom-call | tf_op jit(solution)/shard_map/deliver/pallas_call | solution.py:200
  207.0 0.5 copy.36
  207.6 1.2 convolution_convert_fusion.1
  (6 shorter events, 0.0 us)
Async XLA Ops:
  6.5 3.2 %copy-start = (bf16[256,1024]{1,0:T(8,128)(2,1)S(1)}, bf16[256,1024]{1,0:T(8,128)(2,1)}, u32[]{:S(2)}) copy-start(bf16[256,1024]{1,0:T(8,128)(2,1)} %param.8) | copy-start | bytes 1572868
  6.5 4.2 %copy-start.1 = (bf16[256,1024]{1,0:T(8,128)(2,1)S(1)}, bf16[256,1024]{1,0:T(8,128)(2,1)}, u32[]{:S(2)}) copy-start(bf16[256,1024]{1,0:T(8,128)(2,1)} %param.9) | copy-start | bytes 1572868
  6.5 150.8 %all-gather.2.cloned.1.call-start = ((), (), s32[]{:S(2)}) async-start(), calls=%async_computation | async-start | bytes 6684672 | tf_op jit(solution)/shard_map/all_gather | solution.py:248
  94.0 1.9 copy-start.3
  168.0 39.6 %copy-start.2 = (bf16[512,256]{1,0:T(8,128)(2,1)S(1)}, bf16[512,256]{1,0:T(8,128)(2,1)}, u32[]{:S(2)}) copy-start(bf16[512,256]{1,0:T(8,128)(2,1)} %constant.2.clone) | copy-start | bytes 786436
Sparse Core Ops, SparseCore 0:
  9.8 132.7 all-gather.1

commit v4 on v3

--- a/solution.py
+++ b/solution.py
@@ -20,63 +20,64 @@
     return lax.axis_index("z"), lax.axis_index("y"), lax.axis_index("x")
 
 
-def swap_kernel(src, dst, send_sem, recv_sem, own_sem):
-    z, y, x = position()
-    me = z * 16 + y * 4 + x
+def tm_peer(place, step):
+    z, y, x = place
+    return {
+        "z": (z + step // 16) % 4,
+        "y": (y + (step // 4) % 4) % 4,
+        "x": (x + step % 4) % 4,
+    }
+
+
+def tm_index(at):
+    return at["z"] * 16 + at["y"] * 4 + at["x"]
+
+
+def greet_all(place):
+    barrier = pltpu.get_barrier_semaphore()
+
+    def greet(step, carry):
+        pl.semaphore_signal(
+            barrier, inc=1, device_id=tm_peer(place, step), device_id_type=BY_MESH
+        )
+        return carry
+
+    lax.fori_loop(1, 64, greet, 0)
+    pl.semaphore_wait(barrier, 63)
+
+
+def swap_start(place, src, dst, send_sem, recv_sem, own_sem):
+    me = tm_index(tm_peer(place, 0))
     own = pltpu.make_async_copy(src.at[me], dst.at[me], own_sem)
     own.start()
-    barrier = pltpu.get_barrier_semaphore()
-
-    def peer(step):
-        return (z + step // 16) % 4, (y + (step // 4) % 4) % 4, (x + step % 4) % 4
-
-    def greet(step, carry):
-        pl.semaphore_signal(barrier, inc=1, device_id=dict(zip(TM, peer(step))), device_id_type=BY_MESH)
-        return carry
-
-    lax.fori_loop(1, 64, greet, 0)
-    pl.semaphore_wait(barrier, 63)
 
     def send(step, carry):
-        pz, py, px = peer(step)
+        to = tm_peer(place, step)
         pltpu.make_async_remote_copy(
-            src_ref=src.at[pz * 16 + py * 4 + px],
+            src_ref=src.at[tm_index(to)],
             dst_ref=dst.at[me],
             send_sem=send_sem,
             recv_sem=recv_sem,
-            device_id={"z": pz, "y": py, "x": px},
+            device_id=to,
             device_id_type=BY_MESH,
         ).start()
         return carry
 
     lax.fori_loop(1, 64, send, 0)
+    return own
+
+
+def swap_wait(own, src, dst, send_sem, recv_sem):
     most = pl.ds(0, 63)
     pltpu.make_async_copy(src.at[most], src.at[most], send_sem).wait()
     pltpu.make_async_copy(dst.at[most], dst.at[most], recv_sem).wait()
     own.wait()
 
 
-def swap(array, collective_id):
-    return pl.pallas_call(
-        swap_kernel,
-        out_shape=jax.ShapeDtypeStruct(array.shape, array.dtype),
-        in_specs=[ANY],
-        out_specs=ANY,
-        scratch_shapes=[pltpu.SemaphoreType.DMA] * 3,
-        compiler_params=pltpu.CompilerParams(collective_id=collective_id, has_side_effects=True),
-        name=f"swap_{collective_id}",
-    )(array)
-
-
-def share_kernel(src, dst, send_sem, recv_sem, own_sem):
-    y = lax.axis_index("y")
+def share_start(y, src, dst, send_sem, recv_sem, own_sem):
     up, down = (y + 1) % 4, (y + 3) % 4
     own = pltpu.make_async_copy(src, dst.at[:, y], own_sem)
     own.start()
-    barrier = pltpu.get_barrier_semaphore()
-    for target in (up, down):
-        pl.semaphore_signal(barrier, inc=1, device_id={"y": target}, device_id_type=BY_MESH)
-    pl.semaphore_wait(barrier, 2)
 
     def send(block, slot, c, target, lane):
         copy = pltpu.make_async_remote_copy(
@@ -90,41 +91,129 @@
         copy.start()
         return copy
 
-    ups, downs, far = {}, {}, []
+    ups, downs = {}, {}
     for step in range(4):
         c, d = step, (step + 2) % 4
         ups[c] = send(src.at[:, c], y, c, up, 0)
         downs[d] = send(src.at[:, d], y, d, down, 1)
-    for step in range(2):
-        c, d = step, step + 2
-        ups[c].wait_recv()
-        far.append(send(dst.at[:, down, c], down, c, up, 2))
-        downs[d].wait_recv()
-        far.append(send(dst.at[:, up, d], up, d, down, 2))
-    for step in range(2):
-        ups[step + 2].wait_recv()
-        downs[step].wait_recv()
-    for copy in far:
-        copy.wait_recv()
-    for copy in (*ups.values(), *downs.values(), *far):
-        copy.wait_send()
-    own.wait()
-
-
-def share(grads):
-    m, c, f, k = grads.shape
+
+    def finish():
+        far = []
+        for step in range(2):
+            c, d = step, step + 2
+            ups[c].wait_recv()
+            far.append(send(dst.at[:, down, c], down, c, up, 2))
+            downs[d].wait_recv()
+            far.append(send(dst.at[:, up, d], up, d, down, 2))
+        for step in range(2):
+            ups[step + 2].wait_recv()
+            downs[step].wait_recv()
+        for copy in far:
+            copy.wait_recv()
+        for copy in (*ups.values(), *downs.values(), *far):
+            copy.wait_send()
+        own.wait()
+
+    return finish
+
+
+def first_kernel(query, key_in, value, grad_out, moved, later, packed, *swap_sems):
+    place = position()
+    width = moved.shape[-1]
+    greet_all(place)
+    row = lax.broadcasted_iota(jnp.int32, (64, 64), 0)
+    column = lax.broadcasted_iota(jnp.int32, (64, 64), 1)
+    wanted = ((row // 4) % 4) * 16 + (row // 16) * 4 + row % 4
+    order = jnp.where(column == wanted, 1.0, 0.0).astype(BF16)
+
+    def pack(into, columns):
+        def body(group, carry):
+            rows = pl.ds(pl.multiple_of(group * 16, 16), 16)
+            block = jnp.concatenate(
+                [ref[rows, columns] for ref in (query, key_in, value, grad_out)], axis=0
+            )
+            ordered = jnp.dot(order, block, preferred_element_type=F32).astype(BF16)
+            into[pl.ds(group * 4, 4)] = ordered.reshape(4, 16, width)
+            return carry
+
+        lax.fori_loop(0, 16, body, 0)
+
+    pack(packed, pl.ds(0, width))
+    own = swap_start(place, packed, moved, *swap_sems)
+    pack(later, pl.ds(width, width))
+    swap_wait(own, packed, moved, *swap_sems[:2])
+
+
+def second_kernel(src, grads, moved, shared, *sems):
+    place = position()
+    greet_all(place)
+    finish = share_start(place[1], grads, shared, *sems[3:])
+    own = swap_start(place, src, moved, *sems[:3])
+    finish()
+    swap_wait(own, src, moved, *sems[:2])
+
+
+def third_kernel(grads, shared, *sems):
+    y = lax.axis_index("y")
+    barrier = pltpu.get_barrier_semaphore()
+    for step in (1, 3):
+        pl.semaphore_signal(barrier, inc=1, device_id={"y": (y + step) % 4}, device_id_type=BY_MESH)
+    pl.semaphore_wait(barrier, 2)
+    share_start(y, grads, shared, *sems)()
+
+
+SWAP_SEMS = [pltpu.SemaphoreType.DMA] * 3
+SHARE_SEMS = [
+    pltpu.SemaphoreType.DMA((3, 4)),
+    pltpu.SemaphoreType.DMA((3, 4)),
+    pltpu.SemaphoreType.DMA,
+]
+VMEM = pl.BlockSpec(memory_space=pltpu.VMEM)
+
+
+def params(collective_id):
+    return pltpu.CompilerParams(
+        collective_id=collective_id, has_side_effects=True, vmem_limit_bytes=24 << 20
+    )
+
+
+def first(*arrays):
+    block = jax.ShapeDtypeStruct((64, 16, 512), BF16)
     return pl.pallas_call(
-        share_kernel,
-        out_shape=jax.ShapeDtypeStruct((m, 4, c, f, k), grads.dtype),
+        first_kernel,
+        out_shape=(block, block),
+        in_specs=[VMEM] * 4,
+        out_specs=(ANY, VMEM),
+        scratch_shapes=[pltpu.VMEM(block.shape, BF16), *SWAP_SEMS],
+        compiler_params=params(1),
+        name="swap_first",
+    )(*arrays)
+
+
+def second(src, grads):
+    return pl.pallas_call(
+        second_kernel,
+        out_shape=(
+            jax.ShapeDtypeStruct(src.shape, BF16),
+            jax.ShapeDtypeStruct((3, 4, 4, 64, 512), BF16),
+        ),
+        in_specs=[ANY, ANY],
+        out_specs=(ANY, ANY),
+        scratch_shapes=[*SWAP_SEMS, *SHARE_SEMS],
+        compiler_params=params(3),
+        name="swap_and_share",
+    )(src, grads)
+
+
+def third(grads):
+    return pl.pallas_call(
+        third_kernel,
+        out_shape=jax.ShapeDtypeStruct((3, 4, 4, 64, 512), BF16),
         in_specs=[ANY],
         out_specs=ANY,
-        scratch_shapes=[
-            pltpu.SemaphoreType.DMA((3, 4)),
-            pltpu.SemaphoreType.DMA((3, 4)),
-            pltpu.SemaphoreType.DMA,
-        ],
-        compiler_params=pltpu.CompilerParams(collective_id=3, has_side_effects=True),
-        name="share",
+        scratch_shapes=SHARE_SEMS,
+        compiler_params=params(4),
+        name="share_last",
     )(grads)
 
 
@@ -135,11 +224,7 @@
     barrier = pltpu.get_barrier_semaphore()
 
     def peer(step):
-        return {
-            "z": (z + step // 16) % 4,
-            "y": (y + (step // 4) % 4) % 4,
-            "x": (x + step % 4) % 4,
-        }
+        return tm_peer((z, y, x), step)
 
     def greet(first, half):
         def body(step, carry):
@@ -176,7 +261,7 @@
         def send(step, carry):
             to = peer(step)
             pltpu.make_async_remote_copy(
-                src_ref=total.at[at, to["z"] * 16 + to["y"] * 4 + to["x"]],
+                src_ref=total.at[at, tm_index(to)],
                 dst_ref=dst.at[slot],
                 send_sem=send_sem,
                 recv_sem=recv_sem,
@@ -211,9 +296,7 @@
             pltpu.SemaphoreType.DMA,
             pltpu.SemaphoreType.DMA,
         ],
-        compiler_params=pltpu.CompilerParams(
-            collective_id=2, has_side_effects=True, vmem_limit_bytes=24 << 20
-        ),
+        compiler_params=params(2),
         name="deliver",
     )(part)
 
@@ -244,17 +327,31 @@
     return grad_query.astype(BF16), grad_key.astype(BF16), grad_value.astype(BF16)
 
 
+def gradients(moved):
+    moved = moved.reshape(64, 4, 4, 4, HD)
+    grads = temporal(moved[:, 0], moved[:, 1], moved[:, 2], moved[:, 3])
+    return jnp.stack([a.reshape(4, 64, 512) for a in grads])
+
+
+def product(shared, rows):
+    return jnp.einsum(
+        "mtk,mzik->zti",
+        shared.reshape(3, 1024, 512),
+        rows.reshape(3, 4, 256, 512),
+        preferred_element_type=F32,
+    )
+
+
 def per_device(query, key_in, value, grad_out, weights):
-    rows = lax.all_gather(weights, ("z", "x"), axis=1, tiled=True)
-    packed = jnp.stack([a.reshape(64, 4, 1024) for a in (query, key_in, value, grad_out)], axis=1)
-    moved = swap(packed.reshape(64, 16, 1024), 1).reshape(64, 4, 4, 8, HD)
-    grads = temporal(moved[:, 0], moved[:, 1], moved[:, 2], moved[:, 3])
-    stacked = jnp.stack([a.reshape(4, 64, 1024) for a in grads])
-    shared = share(stacked).reshape(3, 1024, 1024)
-    partial_sum = jnp.einsum(
-        "mtk,mzik->zti", shared, rows.reshape(3, 4, 256, 1024), preferred_element_type=F32
-    ).astype(BF16)
-    back = deliver(partial_sum).reshape(4, 512, 256)
+    rows = [
+        lax.all_gather(weights[:, :, at : at + 512], ("z", "x"), axis=1, tiled=True)
+        for at in (0, 512)
+    ]
+    moved, later = first(query, key_in, value, grad_out)
+    moved, shared = second(later, gradients(moved))
+    grads = gradients(moved)
+    partial_sum = product(shared, rows[0]) + product(third(grads), rows[1])
+    back = deliver(partial_sum.astype(BF16)).reshape(4, 512, 256)
     place = jnp.asarray(patch_order(), BF16)
     out = jnp.einsum("ytk,tp->ykp", back, place, preferred_element_type=F32)
     return out.reshape(1024, 256).astype(BF16)

time: 218 us -> 241 us (1.11); the launches traced: 216 us -> 241 us
  waiting for transfers between devices: 0.73 us -> 26.7 us
  other arithmetic: 4 us -> 0.18 us
    all_gather x1 -> x2, waiting for transfers between devices: 0.02 us -> 26 us  [per_device(): lax.all_gather(weights[:, :, at:at + 512], ('z', 'x'), axis=1, tiled=True)]
    another operation x7 -> x6, local copies, waits for them, and re-layouts: 5.13 us -> 0.63 us  [gradients(): return jnp.stack([a.reshape(4, 64, 512) for a in grads])]
    another operation x2, other arithmetic: 4 us -> 0.18 us  [gradients(): return jnp.stack([a.reshape(4, 64, 512) for a in grads])]
    dot_general x1 -> x2, matrix products: 10.7 us -> 14.4 us  [product(): jnp.einsum('mtk,mzik->zti', shared.reshape(3, 1024, 512), rows.reshape(3,...]
    unnamed x9 -> x12, local copies, waits for them, and re-layouts: 2.23 us -> 5.9 us
    pallas_call x2 -> x3, Pallas kernels: 129 us -> 130 us  [the longest x1 54 us: second(): pl.pallas_call(second_kernel, out_shape=(jax.ShapeDtypeStruct(src.shape,...]
  transfers between devices with their start and end apart: 1 -> 2, of which waited for: 0 -> 1; matrix products, arithmetic and copies ran while one was open for 10% -> 6% of each run, Pallas kernels for 60% -> 54%
where the time goes in v4:
time: 241 us
  Pallas kernels  170 us (71%)
  waiting for transfers between devices  26.7 us (11%)
  matrix products  19.2 us (8%)
  between operations  13.7 us (6%)
  local copies, waits for them, and re-layouts  11.4 us (5%)
    pallas_call x1, Pallas kernels, second(): pl.pallas_call(second_kernel, out_shape=(jax.ShapeDtypeStruct(src.shape,...  54 us
    pallas_call x1, Pallas kernels, first(): pl.pallas_call(first_kernel, out_shape=(block, block), in_specs=[VMEM] *...  48.6 us
    pallas_call x1, Pallas kernels, deliver(): pl.pallas_call(deliver_kernel, out_shape=jax.ShapeDtypeStruct((128, 16, 2...  40.3 us
    pallas_call x1, Pallas kernels, third(): pl.pallas_call(third_kernel, out_shape=jax.ShapeDtypeStruct((3, 4, 4, 64,...  27 us
    all_gather x2, waiting for transfers between devices, per_device(): lax.all_gather(weights[:, :, at:at + 512], ('z', 'x'), axis=1, tiled=True)  26 us
    dot_general x2, matrix products, product(): jnp.einsum('mtk,mzik->zti', shared.reshape(3, 1024, 512), rows.reshape(3,...  14.4 us
    unnamed x12, local copies, waits for them, and re-layouts  5.9 us
  transfers between devices with their start and end apart: 2, of which 1 were waited for; matrix products, arithmetic and copies ran while one was open for 6% of the time, Pallas kernels for 54%

profile of v4, /device:TPU:1, one launch (start us, length us, event | category | flops | bytes accessed | tf_op | source)
XLA Modules:
  0.0 241.1 jit_solution(10561816173933439733)
XLA Ops:
  6.5 1.8 fusion.38
  8.4 0.7 all-gather.5.cloned.1.call-update
  9.1 1.0 copy-done
  10.2 1.0 copy-done.1
  11.2 1.0 copy-done.2
  12.2 1.0 copy-done.3
  13.3 48.6 %swap_first.1 = (bf16[64,16,512]{2,1,0:T(8,128)(2,1)S(1)}, bf16[64,16,512]{2,1,0:T(8,128)(2,1)S(1)}) custom-call(bf16[256,1024]{1,0:T(8,128)(2,1)S(1)} %copy-done, bf16[256,1024]{1,0:T(8,128)(2,1)S(1)} %copy-done.1, bf16[256,1024]{1,0:T(8,128)(2,1)S(1)} %copy-done.2, bf16[256,1024]{1,0:T(8,128)(2,1)S(1)} %copy-done.3), custom_call_target="tpu_custom_call" | custom-call | tf_op jit(solution)/shard_map/swap_first/pallas_call | solution.py:182
  61.9 0.3 reshape.29
  62.2 0.4 fusion.37
  62.6 0.3 fusion.39
  62.9 0.4 fusion.19
  63.4 0.3 fusion.12
  63.7 0.3 fusion.23
  64.3 0.2 fusion.21
  64.8 0.2 fusion.24
  65.5 54.0 %swap_and_share.1 = (bf16[64,16,512]{2,1,0:T(8,128)(2,1)S(1)}, bf16[3,4,4,64,512]{4,3,2,1,0:T(8,128)(2,1)S(1)}) custom-call(bf16[64,16,512]{2,1,0:T(8,128)(2,1)S(1)} %get-tuple-element.9.src, bf16[3,4,64,512]{3,2,1,0:T(8,128)(2,1)S(1)} %pad_maximum_fusion.grads), custom_call_target="tpu_custom_call" | custom-call | tf_op jit(solution)/shard_map/swap_and_share/pallas_call | solution.py:194
  119.4 1.7 copy-done.4
  121.2 0.3 reshape.32
  121.5 0.4 fusion.36
  121.8 0.3 fusion.40
  122.2 0.4 fusion.18
  122.6 0.3 fusion.13
  122.9 0.3 fusion.22
  123.5 0.2 fusion.20
  124.0 0.2 fusion.25
  124.7 27.0 %share_last.1 = bf16[3,4,4,64,512]{4,3,2,1,0:T(8,128)(2,1)S(1)} custom-call(bf16[3,4,64,512]{3,2,1,0:T(8,128)(2,1)S(1)} %pad_maximum_fusion.1.grads), custom_call_target="tpu_custom_call" | custom-call | tf_op jit(solution)/shard_map/share_last/pallas_call | solution.py:209
  151.8 8.2 %fusion.41 = f32[1024,4,256,1]{2,0,1,3:T(8,128)} fusion(bf16[3,1024,512,1]{2,1,3,0:T(8,128)(2,1)} %bitcast.132, bf16[3,4,256,512]{3,2,1,0:T(8,128)(2,1)} %bitcast.134), kind=kOutput, calls=%fused_computation.63 | convolution fusion | flops 3221225472 | bytes 10485760 | tf_op jit(solution)/shard_map/mtk,mzik->zti/dot_general | solution.py:337
  160.0 26.0 %all-gather.5.cloned.1.call-done = bf16[3,1024,512]{2,1,0:T(8,128)(2,1)} async-done(((bf16[3,64,512]{2,1,0:T(8,128)(2,1)}), bf16[3,1024,512]{2,1,0:T(8,128)(2,1)}) %all-gather.5.cloned.1.call-update) | async-done | bytes 3145744 | tf_op jit(solution)/shard_map/all_gather | solution.py:347
  186.0 6.2 %fusion.3.part = bf16[4,1024,256]{2,1,0:T(8,128)(2,1)S(1)} fusion(bf16[3,1024,512,1]{2,1,3,0:T(8,128)(2,1)S(1)} %bitcast.131, bf16[3,4,256,512]{3,2,1,0:T(8,128)(2,1)} %bitcast.135, f32[1024,4,256,1]{2,0,1,3:T(8,128)} %fusion.41), kind=kOutput, calls=%fused_computation.4 | convolution fusion | flops 3223322624 | bytes 12582912 | tf_op jit(solution)/shard_map/mtk,mzik->zti/dot_general | solution.py:337
  192.2 40.3 %deliver.1 = bf16[128,16,256]{2,1,0:T(8,128)(2,1)S(1)} custom-call(bf16[4,1024,256]{2,1,0:T(8,128)(2,1)S(1)} %fusion.3.part), custom_call_target="tpu_custom_call" | custom-call | tf_op jit(solution)/shard_map/deliver/pallas_call | solution.py:285
  232.5 0.5 copy.49
  233.0 1.2 convolution_convert_fusion
  (25 shorter events, 2.1 us)
Async XLA Ops:
  6.5 145.2 %all-gather.3.cloned.1.call-start = ((), (), s32[]{:S(2)}) async-start(), calls=%async_computation | async-start | bytes 3342336 | tf_op jit(solution)/shard_map/all_gather | solution.py:347
  8.4 177.6 %all-gather.5.cloned.1.call-start = ((), (), s32[]{:S(2)}) async-start(), calls=%async_computation.1 | async-start | bytes 3342336 | tf_op jit(solution)/shard_map/all_gather | solution.py:347
  9.1 1.0 copy-start
  10.2 1.0 copy-start.1
  11.2 1.0 copy-start.2
  12.2 1.0 copy-start.3
  119.4 1.7 copy-start.4
  192.2 40.9 %copy-start.5 = (bf16[512,256]{1,0:T(8,128)(2,1)S(1)}, bf16[512,256]{1,0:T(8,128)(2,1)}, u32[]{:S(2)}) copy-start(bf16[512,256]{1,0:T(8,128)(2,1)} %constant.2.clone) | copy-start | bytes 786436
Sparse Core Ops, SparseCore 0:
  9.8 100.6 all-gather.2
  112.9 72.9 all-gather.4

commit v5 on v4

v5 whole, which is shorter than its diff:
```python
import jax
import jax.numpy as jnp
import numpy as np
from jax import lax
from jax.experimental import pallas as pl
from jax.experimental.pallas import tpu as pltpu
from jax.sharding import Mesh, PartitionSpec as P

HD = 128
WIDTH = 512
AXES = ("z", "y", "x", "zl", "c")
TM = AXES[:3]
HEAD = AXES[3:]
BF16 = jnp.bfloat16
F32 = jnp.float32
BY_MESH = pl.DeviceIdType.MESH
ANY = pl.BlockSpec(memory_space=pl.ANY)


def position():
    return lax.axis_index("z"), lax.axis_index("y"), lax.axis_index("x")


def tm_peer(place, step):
    z, y, x = place
    return {
        "z": (z + step // 16) % 4,
        "y": (y + (step // 4) % 4) % 4,
        "x": (x + step % 4) % 4,
    }


def tm_index(at):
    return at["z"] * 16 + at["y"] * 4 + at["x"]


def greet_all(place):
    barrier = pltpu.get_barrier_semaphore()

    def greet(step, carry):
        pl.semaphore_signal(
            barrier, inc=1, device_id=tm_peer(place, step), device_id_type=BY_MESH
        )
        return carry

    lax.fori_loop(1, 64, greet, 0)
    pl.semaphore_wait(barrier, 63)


def swap_start(place, src, dst, send_sem, recv_sem, own_sem):
    me = tm_index(tm_peer(place, 0))
    own = pltpu.make_async_copy(src.at[me], dst.at[me], own_sem)
    own.start()

    def send(step, carry):
        to = tm_peer(place, step)
        pltpu.make_async_remote_copy(
            src_ref=src.at[tm_index(to)],
            dst_ref=dst.at[me],
            send_sem=send_sem,
            recv_sem=recv_sem,
            device_id=to,
            device_id_type=BY_MESH,
        ).start()
        return carry

    lax.fori_loop(1, 64, send, 0)
    return own


def swap_wait(own, src, dst, send_sem, recv_sem):
    most = pl.ds(0, 63)
    pltpu.make_async_copy(src.at[most], src.at[most], send_sem).wait()
    pltpu.make_async_copy(dst.at[most], dst.at[most], recv_sem).wait()
    own.wait()


def share_start(y, src, dst, columns, send_sem, recv_sem, own_sem):
    up, down = (y + 1) % 4, (y + 3) % 4
    own = pltpu.make_async_copy(
        src.at[:, :, :, columns], dst.at[:, y, :, :, columns], own_sem
    )
    own.start()

    def send(block, slot, c, target, lane):
        copy = pltpu.make_async_remote_copy(
            src_ref=block,
            dst_ref=dst.at[:, slot, c, :, columns],
            send_sem=send_sem.at[lane, c],
            recv_sem=recv_sem.at[lane, c],
            device_id={"y": target},
            device_id_type=BY_MESH,
        )
        copy.start()
        return copy

    ups, downs = {}, {}
    for step in range(4):
        c, d = step, (step + 2) % 4
        ups[c] = send(src.at[:, c, :, columns], y, c, up, 0)
        downs[d] = send(src.at[:, d, :, columns], y, d, down, 1)

    far = []

    def forward():
        for step in range(2):
            c, d = step, step + 2
            ups[c].wait_recv()
            far.append(send(dst.at[:, down, c, :, columns], down, c, up, 2))
            downs[d].wait_recv()
            far.append(send(dst.at[:, up, d, :, columns], up, d, down, 2))

    def finish():
        for step in range(2):
            ups[step + 2].wait_recv()
            downs[step].wait_recv()
        for copy in far:
            copy.wait_recv()
        for copy in (*ups.values(), *downs.values(), *far):
            copy.wait_send()
        own.wait()

    return forward, finish


def pack(arrays, into, columns):
    row = lax.broadcasted_iota(jnp.int32, (64, 64), 0)
    column = lax.broadcasted_iota(jnp.int32, (64, 64), 1)
    wanted = ((row // 4) % 4) * 16 + (row // 16) * 4 + row % 4
    order = jnp.where(column == wanted, 1.0, 0.0).astype(BF16)

    def body(group, carry):
        rows = pl.ds(pl.multiple_of(group * 16, 16), 16)
        block = jnp.concatenate([ref[rows, columns] for ref in arrays], axis=0)
        ordered = jnp.dot(order, block, preferred_element_type=F32).astype(BF16)
        into[pl.ds(group * 4, 4)] = ordered.reshape(4, 16, WIDTH)
        return carry

    lax.fori_loop(0, 16, body, 0)


def attend(moved, heads, grads, chunk):
    heads[...] = pltpu.einshape("abk->bak", moved[...].astype(F32)).astype(BF16)
    scale = 1.0 / HD**0.5
    row = lax.broadcasted_iota(jnp.int32, (128, 128), 0)
    column = lax.broadcasted_iota(jnp.int32, (128, 128), 1)
    same = row // 64 == column // 64

    def dot(a, b, over_a, over_b):
        return lax.dot_general(
            a, b, (((over_a,), (over_b,)), ((), ())), preferred_element_type=F32
        )

    def body(pair, carry):
        patches = pl.ds(pair * 2, 2)
        for head in range(WIDTH // HD):
            lanes = slice(head * HD, (head + 1) * HD)
            q, k, v, g = (
                heads[pl.ds(array * 4 + pair * 2, 2), :, lanes].reshape(128, HD)
                for array in range(4)
            )
            scores = jnp.where(same, dot(q, k, 1, 1) * scale, -1e30)
            weight = jnp.exp(scores - jnp.max(scores, axis=1, keepdims=True))
            probs = weight / jnp.sum(weight, axis=1, keepdims=True)
            probs_b = probs.astype(BF16)
            attended = dot(probs_b, v, 1, 0)
            delta = jnp.sum(g.astype(F32) * attended, axis=1, keepdims=True)
            grad_scores = (probs * (dot(g, v, 1, 1) - delta)).astype(BF16)
            results = (
                dot(grad_scores, k, 1, 0) * scale,
                dot(grad_scores, q, 0, 0) * scale,
                dot(probs_b, g, 0, 0),
            )
            out = pl.ds(chunk * WIDTH + head * HD, HD)
            for m, result in enumerate(results):
                grads[m, patches, :, out] = result.astype(BF16).reshape(2, 64, HD)
        return carry

    lax.fori_loop(0, 2, body, 0)


def rows_start(place, own_rows, rows, send_sem, recv_sem, own_sem):
    z, y, x = place
    steps = (0, 3, 2, 1)

    def block(b, at_x, part=slice(None)):
        return rows.at[:, ((z + steps[b]) % 4) * 4 + at_x, part]

    def send(src, dst, axis, target, lane, b):
        copy = pltpu.make_async_remote_copy(
            src_ref=src,
            dst_ref=dst,
            send_sem=send_sem.at[lane, b],
            recv_sem=recv_sem.at[lane, b],
            device_id={axis: target},
            device_id_type=BY_MESH,
        )
        copy.start()
        return copy

    z_up, z_down, x_up, x_down = (z + 1) % 4, (z + 3) % 4, (x + 1) % 4, (x + 3) % 4
    own = pltpu.make_async_copy(own_rows, block(0, x), own_sem)
    own.start()
    z_ups = send(own_rows, block(0, x), "z", z_up, 0, 0)
    z_downs = send(own_rows, block(0, x), "z", z_down, 0, 1)
    z_far, ups, downs, far = [], {}, {}, {}

    def along_x(b):
        src = own_rows if b == 0 else block(b, x)
        ups[b] = send(src, block(b, x), "x", x_up, 1, b)
        downs[b] = send(src, block(b, x), "x", x_down, 2, b)

    along_x(0)

    def near():
        low, high = pl.ds(0, 32), pl.ds(32, 32)
        z_ups.wait_recv()
        z_far.append(send(block(1, x, low), block(1, x, low), "z", z_up, 0, 2))
        along_x(1)
        z_downs.wait_recv()
        z_far.append(send(block(3, x, high), block(3, x, high), "z", z_down, 0, 3))
        along_x(3)

    def across():
        for copy in z_far:
            copy.wait_recv()
        along_x(2)

    def forward(b):
        if b < 2:
            ups[b].wait_recv()
            far[b] = send(block(b, x_down), block(b, x_down), "x", x_up, 3, b)
        else:
            downs[b].wait_recv()
            far[b] = send(block(b, x_up), block(b, x_up), "x", x_down, 3, b)

    def finish():
        for b in range(4):
            (downs if b < 2 else ups)[b].wait_recv()
            far[b].wait_recv()
        for copy in (z_ups, z_downs, *z_far, *ups.values(), *downs.values(), *far.values()):
            copy.wait_send()
        own.wait()

    return near, across, forward, finish


def front_kernel(
    query, key_in, value, grad_out, own_rows, shared, rows, packed, moved, heads, grads, *sems
):
    place = position()
    arrays = (query, key_in, value, grad_out)
    swap_sems, share_sems, rows_sems = (sems[:3], sems[3:6]), (sems[6:9], sems[9:12]), sems[12:]
    greet_all(place)
    near, across, pass_on, rows_finish = rows_start(place, own_rows, rows, *rows_sems)
    swaps = []
    for chunk in range(2):
        pack(arrays, packed.at[chunk], pl.ds(chunk * WIDTH, WIDTH))
        swaps.append(swap_start(place, packed.at[chunk], moved.at[chunk], *swap_sems[chunk]))

    def swapped(chunk):
        swap_wait(swaps[chunk], packed.at[chunk], moved.at[chunk], *swap_sems[chunk][:2])
        attend(moved.at[chunk], heads, grads, chunk)
        columns = pl.ds(chunk * WIDTH, WIDTH)
        return share_start(place[1], grads, shared, columns, *share_sems[chunk])

    near()
    forward, share_finish = swapped(0)
    pass_on(0)
    across()
    forward()
    pass_on(1)
    pass_on(3)
    last_forward, last_finish = swapped(1)
    pass_on(2)
    last_forward()
    share_finish()
    last_finish()
    rows_finish()


SWAP_SEMS = [pltpu.SemaphoreType.DMA] * 3
SHARE_SEMS = [
    pltpu.SemaphoreType.DMA((3, 4)),
    pltpu.SemaphoreType.DMA((3, 4)),
    pltpu.SemaphoreType.DMA,
]
ROWS_SEMS = [
    pltpu.SemaphoreType.DMA((4, 4)),
    pltpu.SemaphoreType.DMA((4, 4)),
    pltpu.SemaphoreType.DMA,
]
VMEM = pl.BlockSpec(memory_space=pltpu.VMEM)


def params(collective_id):
    return pltpu.CompilerParams(
        collective_id=collective_id, has_side_effects=True, vmem_limit_bytes=32 << 20
    )


def front(*arrays):
    return pl.pallas_call(
        front_kernel,
        out_shape=(
            jax.ShapeDtypeStruct((3, 4, 4, 64, 2 * WIDTH), BF16),
            jax.ShapeDtypeStruct((3, 16, 64, 2 * WIDTH), BF16),
        ),
        in_specs=[VMEM] * 4 + [ANY],
        out_specs=(ANY, ANY),
        scratch_shapes=[
            pltpu.VMEM((2, 64, 16, WIDTH), BF16),
            pltpu.VMEM((2, 64, 16, WIDTH), BF16),
            pltpu.VMEM((16, 64, WIDTH), BF16),
            pltpu.VMEM((3, 4, 64, 2 * WIDTH), BF16),
            *SWAP_SEMS,
            *SWAP_SEMS,
            *SHARE_SEMS,
            *SHARE_SEMS,
            *ROWS_SEMS,
        ],
        compiler_params=params(1),
        name="front",
    )(*arrays)


def deliver_kernel(part, dst, other, total, core_send, core_recv, send_sem, recv_sem, own_sem):
    z, y, x = position()
    zl, core = lax.axis_index("zl"), lax.axis_index("c")
    slot = ((y * 4 + z) * 4 + x) * 2 + zl
    barrier = pltpu.get_barrier_semaphore()

    def peer(step):
        return tm_peer((z, y, x), step)

    def greet(first, half):
        def body(step, carry):
            pl.semaphore_signal(
                barrier, inc=1, device_id={**peer(step), "zl": half}, device_id_type=BY_MESH
            )
            return carry

        lax.fori_loop(first, 64, body, 0)

    pl.semaphore_signal(barrier, inc=1, device_id={"c": 1 - core}, device_id_type=BY_MESH)
    greet(0, 1 - zl)
    greet(1, zl)
    pl.semaphore_wait(barrier, 128)

    halves = (1 - zl, zl)
    copies = []
    for at, half in enumerate(halves):
        copy = pltpu.make_async_remote_copy(
            src_ref=part.at[2 * half + 1 - core],
            dst_ref=other.at[at],
            send_sem=core_send.at[at],
            recv_sem=core_recv.at[at],
            device_id={"c": 1 - core},
            device_id_type=BY_MESH,
        )
        copy.start()
        copies.append(copy)
    for at, half in enumerate(halves):
        copies[at].wait_recv()
        both = part[2 * half + core].astype(F32) + other[at].astype(F32)
        total[at] = pltpu.einshape("abk->bak", both.reshape(16, 64, 256)).astype(BF16)

        def send(step, carry):
            to = peer(step)
            pltpu.make_async_remote_copy(
                src_ref=total.at[at, tm_index(to)],
                dst_ref=dst.at[slot],
                send_sem=send_sem,
                recv_sem=recv_sem,
                device_id={**to, "zl": half},
                device_id_type=BY_MESH,
            ).start()
            return carry

        lax.fori_loop(at, 64, send, 0)
    own = pltpu.make_async_copy(total.at[1, z * 16 + y * 4 + x], dst.at[slot], own_sem)
    own.start()
    most = dst.at[pl.ds(0, 127)]
    pltpu.make_async_copy(most, most, send_sem).wait()
    pltpu.make_async_copy(most, most, recv_sem).wait()
    for copy in copies:
        copy.wait_send()
    own.wait()


def deliver(part):
    return pl.pallas_call(
        deliver_kernel,
        out_shape=jax.ShapeDtypeStruct((128, 16, 256), part.dtype),
        in_specs=[pl.BlockSpec(memory_space=pltpu.VMEM)],
        out_specs=ANY,
        scratch_shapes=[
            pltpu.VMEM((2, 1024, 256), part.dtype),
            pltpu.VMEM((2, 64, 16, 256), part.dtype),
            pltpu.SemaphoreType.DMA((2,)),
            pltpu.SemaphoreType.DMA((2,)),
            pltpu.SemaphoreType.DMA,
            pltpu.SemaphoreType.DMA,
            pltpu.SemaphoreType.DMA,
        ],
        compiler_params=params(2),
        name="deliver",
    )(part)


def patch_order():
    z, x, _, slot, c = np.indices((4, 4, 2, 4, 4)).reshape(5, 512)
    return np.eye(256, dtype=np.float32)[4 * (z * 16 + slot * 4 + x) + c]


def per_device(query, key_in, value, grad_out, weights):
    shared, rows = front(query, key_in, value, grad_out, weights)
    partial_sum = jnp.einsum(
        "mtk,mzik->zti",
        shared.reshape(3, 1024, 1024),
        rows.reshape(3, 4, 256, 1024),
        preferred_element_type=F32,
    )
    back = deliver(partial_sum.astype(BF16)).reshape(4, 512, 256)
    place = jnp.asarray(patch_order(), BF16)
    out = jnp.einsum("ytk,tp->ykp", back, place, preferred_element_type=F32)
    return out.reshape(1024, 256).astype(BF16)


def solution(mesh):
    fine = Mesh(mesh.devices.reshape(4, 4, 4, 2, 2), AXES)
    placed = (P(TM, HEAD),) * 4 + (P(None, TM, HEAD),)
    return jax.shard_map(
        per_device, mesh=fine, in_specs=placed, out_specs=P(HEAD, TM), check_vma=False
    )
```

time: 241 us -> 184 us (0.76)
  waiting for transfers between devices: 26.7 us -> 0 us
  between operations: 13.7 us -> 0.05 us
  matrix products: 19.2 us -> 8.15 us
  local copies, waits for them, and re-layouts: 11.4 us -> 5.71 us
    all_gather x2 -> x0, waiting for transfers between devices: 26 us -> none  [per_device(): lax.all_gather(weights[:, :, at:at + 512], ('z', 'x'), axis=1, tiled=True)]
    pallas_call x3 -> x1, Pallas kernels: 130 us -> 113 us  [front(): pl.pallas_call(front_kernel, out_shape=(jax.ShapeDtypeStruct((3, 4, 4, 64...]
    pallas_call x1, Pallas kernels: 40.3 us -> 56.4 us  [deliver(): pl.pallas_call(deliver_kernel, out_shape=jax.ShapeDtypeStruct((128, 16, 2...]
    dot_general x12 -> x1, matrix products: 17.3 us -> 6.92 us  [per_device(): jnp.einsum('mtk,mzik->zti', shared.reshape(3, 1024, 1024), rows.reshape(3...]
    slice x3 -> x0, local copies, waits for them, and re-layouts: 2.52 us -> none  [the longest x1 1.79 us: per_device(): weights[:, :, at:at + 512]]
  transfers between devices with their start and end apart: 2 -> 0, of which waited for: 1 -> 0; matrix products, arithmetic and copies ran while one was open for 6% -> 0% of each run, Pallas kernels for 54% -> 0%
where the time goes in v5:
time: 184 us
  Pallas kernels  170 us (92%)
  matrix products  8.15 us (4%)
  local copies, waits for them, and re-layouts  5.71 us (3%)
    pallas_call x1, Pallas kernels, front(): pl.pallas_call(front_kernel, out_shape=(jax.ShapeDtypeStruct((3, 4, 4, 64...  113 us
    pallas_call x1, Pallas kernels, deliver(): pl.pallas_call(deliver_kernel, out_shape=jax.ShapeDtypeStruct((128, 16, 2...  56.4 us
    dot_general x1, matrix products, per_device(): jnp.einsum('mtk,mzik->zti', shared.reshape(3, 1024, 1024), rows.reshape(3...  6.92 us
    unnamed x12, local copies, waits for them, and re-layouts  5.17 us

profile of v5, /device:TPU:1, one launch (start us, length us, event | category | flops | bytes accessed | tf_op | source)
XLA Modules:
  0.0 183.5 jit_solution(5610776254488597798)
XLA Ops:
  0.0 0.0 copy-start
  0.0 1.0 copy-done
  1.0 0.0 copy-start.1
  1.0 1.0 copy-done.1
  2.1 0.0 copy-start.2
  2.1 1.0 copy-done.2
  3.1 0.0 copy-start.3
  3.1 1.0 copy-done.3
  4.2 0.0 copy-start.4
  4.2 1.0 copy-done.4
  5.2 113.2 %front.1 = (bf16[3,4,4,64,1024]{4,3,2,1,0:T(8,128)(2,1)S(1)}, bf16[3,16,64,1024]{3,2,1,0:T(8,128)(2,1)S(1)}) custom-call(bf16[256,1024]{1,0:T(8,128)(2,1)S(1)} %copy-done, bf16[256,1024]{1,0:T(8,128)(2,1)S(1)} %copy-done.1, bf16[256,1024]{1,0:T(8,128)(2,1)S(1)} %copy-done.2, bf16[256,1024]{1,0:T(8,128)(2,1)S(1)} %copy-done.3, bf16[3,64,1024]{2,1,0:T(8,128)(2,1)S(1)} %copy-done.4), custom_call_target="tpu_custom_call" | custom-call | tf_op jit(solution)/shard_map/front/pallas_call | solution.py:303
  118.4 0.0 copy-start.5
  118.4 6.9 %fusion.part = bf16[4,1024,256]{2,1,0:T(8,128)(2,1)S(1)} fusion(bf16[3,4,256,1024]{3,2,1,0:T(8,128)(2,1)S(1)} %bitcast.22, bf16[3,1024,1024,1]{2,1,3,0:T(8,128)(2,1)S(1)} %bitcast.21), kind=kOutput, calls=%fused_computation.1 | convolution fusion | flops 6443499520 | bytes 14680064 | tf_op jit(solution)/shard_map/mtk,mzik->zti/dot_general | solution.py:418
  125.3 56.4 %deliver.1 = bf16[128,16,256]{2,1,0:T(8,128)(2,1)S(1)} custom-call(bf16[4,1024,256]{2,1,0:T(8,128)(2,1)S(1)} %fusion.part), custom_call_target="tpu_custom_call" | custom-call | tf_op jit(solution)/shard_map/deliver/pallas_call | solution.py:392
  181.8 0.5 copy.11
  182.3 0.0 copy-done.5
  182.3 1.2 convolution_convert_fusion
Async XLA Ops:
  0.0 1.0 copy-start
  1.0 1.0 copy-start.1
  2.1 1.0 copy-start.2
  3.1 1.0 copy-start.3
  4.2 1.0 copy-start.4
  118.4 63.9 %copy-start.5 = (bf16[512,256]{1,0:T(8,128)(2,1)S(1)}, bf16[512,256]{1,0:T(8,128)(2,1)}, u32[]{:S(2)}) copy-start(bf16[512,256]{1,0:T(8,128)(2,1)} %constant.2.clone) | copy-start | bytes 786436

commit v6 on v5

--- a/solution.py
+++ b/solution.py
@@ -7,7 +7,8 @@
 from jax.sharding import Mesh, PartitionSpec as P
 
 HD = 128
-WIDTH = 512
+CHUNKS = 4
+WIDTH = 1024 // CHUNKS
 AXES = ("z", "y", "x", "zl", "c")
 TM = AXES[:3]
 HEAD = AXES[3:]
@@ -131,7 +132,7 @@
 
     def body(group, carry):
         rows = pl.ds(pl.multiple_of(group * 16, 16), 16)
-        block = jnp.concatenate([ref[rows, columns] for ref in arrays], axis=0)
+        block = jnp.concatenate([arrays[at, rows, columns] for at in range(4)], axis=0)
         ordered = jnp.dot(order, block, preferred_element_type=F32).astype(BF16)
         into[pl.ds(group * 4, 4)] = ordered.reshape(4, 16, WIDTH)
         return carry
@@ -246,36 +247,58 @@
 
 
 def front_kernel(
-    query, key_in, value, grad_out, own_rows, shared, rows, packed, moved, heads, grads, *sems
+    query, key_in, value, grad_out, own_rows, shared, rows, local, packed, moved, heads, grads, *sems
 ):
     place = position()
-    arrays = (query, key_in, value, grad_out)
-    swap_sems, share_sems, rows_sems = (sems[:3], sems[3:6]), (sems[6:9], sems[9:12]), sems[12:]
+    sems = list(sems)
+    loads = [
+        pltpu.make_async_copy(ref, local.at[at], sems[0].at[at])
+        for at, ref in enumerate((query, key_in, value, grad_out))
+    ]
+    for load in loads:
+        load.start()
+    rows_sems = sems[1:4]
+    swap_sems = [sems[4 + 3 * chunk : 7 + 3 * chunk] for chunk in range(CHUNKS)]
+    share_sems = [sems[4 + 3 * chunk : 7 + 3 * chunk] for chunk in range(CHUNKS, 2 * CHUNKS)]
     greet_all(place)
+    for load in loads:
+        load.wait()
+    swaps = []
+
+    def swap_out(chunk):
+        pack(local, packed.at[chunk], pl.ds(chunk * WIDTH, WIDTH))
+        swaps.append(swap_start(place, packed.at[chunk], moved.at[chunk], *swap_sems[chunk]))
+
+    swap_out(0)
     near, across, pass_on, rows_finish = rows_start(place, own_rows, rows, *rows_sems)
-    swaps = []
-    for chunk in range(2):
-        pack(arrays, packed.at[chunk], pl.ds(chunk * WIDTH, WIDTH))
-        swaps.append(swap_start(place, packed.at[chunk], moved.at[chunk], *swap_sems[chunk]))
+    for chunk in range(1, CHUNKS):
+        swap_out(chunk)
+    forwards, finishes = [], []
 
     def swapped(chunk):
         swap_wait(swaps[chunk], packed.at[chunk], moved.at[chunk], *swap_sems[chunk][:2])
         attend(moved.at[chunk], heads, grads, chunk)
         columns = pl.ds(chunk * WIDTH, WIDTH)
-        return share_start(place[1], grads, shared, columns, *share_sems[chunk])
-
+        forward, finish = share_start(place[1], grads, shared, columns, *share_sems[chunk])
+        forwards.append(forward)
+        finishes.append(finish)
+
+    swapped(0)
     near()
-    forward, share_finish = swapped(0)
     pass_on(0)
+    forwards[0]()
+    swapped(1)
     across()
-    forward()
+    forwards[1]()
     pass_on(1)
+    swapped(2)
     pass_on(3)
-    last_forward, last_finish = swapped(1)
+    forwards[2]()
+    swapped(3)
     pass_on(2)
-    last_forward()
-    share_finish()
-    last_finish()
+    forwards[3]()
+    for finish in finishes:
+        finish()
     rows_finish()
 
 
@@ -303,21 +326,21 @@
     return pl.pallas_call(
         front_kernel,
         out_shape=(
-            jax.ShapeDtypeStruct((3, 4, 4, 64, 2 * WIDTH), BF16),
-            jax.ShapeDtypeStruct((3, 16, 64, 2 * WIDTH), BF16),
+            jax.ShapeDtypeStruct((3, 4, 4, 64, 1024), BF16),
+            jax.ShapeDtypeStruct((3, 16, 64, 1024), BF16),
         ),
-        in_specs=[VMEM] * 4 + [ANY],
+        in_specs=[pl.BlockSpec(memory_space=pltpu.HBM)] * 5,
         out_specs=(ANY, ANY),
         scratch_shapes=[
-            pltpu.VMEM((2, 64, 16, WIDTH), BF16),
-            pltpu.VMEM((2, 64, 16, WIDTH), BF16),
+            pltpu.VMEM((4, 256, 1024), BF16),
+            pltpu.VMEM((CHUNKS, 64, 16, WIDTH), BF16),
+            pltpu.VMEM((CHUNKS, 64, 16, WIDTH), BF16),
             pltpu.VMEM((16, 64, WIDTH), BF16),
-            pltpu.VMEM((3, 4, 64, 2 * WIDTH), BF16),
-            *SWAP_SEMS,
-            *SWAP_SEMS,
-            *SHARE_SEMS,
-            *SHARE_SEMS,
+            pltpu.VMEM((3, 4, 64, 1024), BF16),
+            pltpu.SemaphoreType.DMA((4,)),
             *ROWS_SEMS,
+            *SWAP_SEMS * CHUNKS,
+            *SHARE_SEMS * CHUNKS,
         ],
         compiler_params=params(1),
         name="front",

time: 184 us -> 182 us (0.989)
  Pallas kernels: 170 us -> 167 us
    pallas_call x1, Pallas kernels: 56.4 us -> 40.2 us  [deliver(): pl.pallas_call(deliver_kernel, out_shape=jax.ShapeDtypeStruct((128, 16, 2...]
    pallas_call x1, Pallas kernels: 113 us -> 127 us  [front(): pl.pallas_call(front_kernel, out_shape=(jax.ShapeDtypeStruct((3, 4, 4, 64...]
where the time goes in v6:
time: 182 us; the launch traced here: 181 us
  Pallas kernels  167 us (92%)
  matrix products  8.14 us (4%)
  local copies, waits for them, and re-layouts  5.71 us (3%)
    pallas_call x1, Pallas kernels, front(): pl.pallas_call(front_kernel, out_shape=(jax.ShapeDtypeStruct((3, 4, 4, 64...  127 us
    pallas_call x1, Pallas kernels, deliver(): pl.pallas_call(deliver_kernel, out_shape=jax.ShapeDtypeStruct((128, 16, 2...  40.2 us
    dot_general x1, matrix products, per_device(): jnp.einsum('mtk,mzik->zti', shared.reshape(3, 1024, 1024), rows.reshape(3...  6.92 us
    unnamed x12, local copies, waits for them, and re-layouts  5.17 us

profile of v6, /device:TPU:1, one launch (start us, length us, event | category | flops | bytes accessed | tf_op | source)
XLA Modules:
  0.0 181.4 jit_solution(7591105256726129352)
XLA Ops:
  0.0 0.0 copy-start
  0.0 1.0 copy-done
  1.0 0.0 copy-start.1
  1.0 1.0 copy-done.1
  2.1 0.0 copy-start.2
  2.1 1.0 copy-done.2
  3.1 0.0 copy-start.3
  3.1 1.0 copy-done.3
  4.2 0.0 copy-start.4
  4.2 1.0 copy-done.4
  5.2 127.3 %front.1 = (bf16[3,4,4,64,1024]{4,3,2,1,0:T(8,128)(2,1)S(1)}, bf16[3,16,64,1024]{3,2,1,0:T(8,128)(2,1)S(1)}) custom-call(bf16[256,1024]{1,0:T(8,128)(2,1)S(1)} %copy-done, bf16[256,1024]{1,0:T(8,128)(2,1)S(1)} %copy-done.1, bf16[256,1024]{1,0:T(8,128)(2,1)S(1)} %copy-done.2, bf16[256,1024]{1,0:T(8,128)(2,1)S(1)} %copy-done.3, bf16[3,64,1024]{2,1,0:T(8,128)(2,1)S(1)} %copy-done.4), custom_call_target="tpu_custom_call" | custom-call | tf_op jit(solution)/shard_map/front/pallas_call | solution.py:326
  132.5 0.0 copy-start.5
  132.5 6.9 %fusion.part = bf16[4,1024,256]{2,1,0:T(8,128)(2,1)S(1)} fusion(bf16[3,4,256,1024]{3,2,1,0:T(8,128)(2,1)S(1)} %bitcast.22, bf16[3,1024,1024,1]{2,1,3,0:T(8,128)(2,1)S(1)} %bitcast.21), kind=kOutput, calls=%fused_computation.1 | convolution fusion | flops 6443499520 | bytes 14680064 | tf_op jit(solution)/shard_map/mtk,mzik->zti/dot_general | solution.py:441
  139.4 40.2 %deliver.1 = bf16[128,16,256]{2,1,0:T(8,128)(2,1)S(1)} custom-call(bf16[4,1024,256]{2,1,0:T(8,128)(2,1)S(1)} %fusion.part), custom_call_target="tpu_custom_call" | custom-call | tf_op jit(solution)/shard_map/deliver/pallas_call | solution.py:415
  179.6 0.5 copy.11
  180.2 0.0 copy-done.5
  180.2 1.2 convolution_convert_fusion
Async XLA Ops:
  0.0 1.0 copy-start
  1.0 1.0 copy-start.1
  2.1 1.0 copy-start.2
  3.1 1.0 copy-start.3
  4.2 1.0 copy-start.4
  132.5 47.7 %copy-start.5 = (bf16[512,256]{1,0:T(8,128)(2,1)S(1)}, bf16[512,256]{1,0:T(8,128)(2,1)}, u32[]{:S(2)}) copy-start(bf16[512,256]{1,0:T(8,128)(2,1)} %constant.2.clone) | copy-start | bytes 786436

commit v7 on v6

--- a/solution.py
+++ b/solution.py
@@ -35,17 +35,21 @@
     return at["z"] * 16 + at["y"] * 4 + at["x"]
 
 
-def greet_all(place):
+def greet_all(place, zl, core):
     barrier = pltpu.get_barrier_semaphore()
 
-    def greet(step, carry):
-        pl.semaphore_signal(
-            barrier, inc=1, device_id=tm_peer(place, step), device_id_type=BY_MESH
-        )
-        return carry
-
-    lax.fori_loop(1, 64, greet, 0)
-    pl.semaphore_wait(barrier, 63)
+    def greet(half):
+        def body(step, carry):
+            to = {**tm_peer(place, step), "zl": half}
+            pl.semaphore_signal(barrier, inc=1, device_id=to, device_id_type=BY_MESH)
+            return carry
+
+        return body
+
+    pl.semaphore_signal(barrier, inc=1, device_id={"c": 1 - core}, device_id_type=BY_MESH)
+    lax.fori_loop(1, 64, greet(zl), 0)
+    lax.fori_loop(0, 64, greet(1 - zl), 0)
+    pl.semaphore_wait(barrier, 128)
 
 
 def swap_start(place, src, dst, send_sem, recv_sem, own_sem):
@@ -246,10 +250,27 @@
     return near, across, forward, finish
 
 
-def front_kernel(
-    query, key_in, value, grad_out, own_rows, shared, rows, local, packed, moved, heads, grads, *sems
+def multiply(shared, rows, hg, slot, first_chunk, chunks):
+    columns = pl.ds(first_chunk * WIDTH, chunks * WIDTH)
+    product = None
+    for m in range(3):
+        term = lax.dot_general(
+            shared[m, slot, :, :, columns].reshape(256, chunks * WIDTH),
+            rows[m, pl.ds(hg * 4, 4), :, columns].reshape(256, chunks * WIDTH),
+            (((1,), (1,)), ((), ())),
+            preferred_element_type=F32,
+        )
+        product = term if product is None else product + term
+    return product
+
+
+def whole_kernel(
+    query, key_in, value, grad_out, own_rows, dst, shared, rows, local, packed, moved, heads, grads,
+    part, leaving, other, total, *sems
 ):
     place = position()
+    z, y, x = place
+    zl, core = lax.axis_index("zl"), lax.axis_index("c")
     sems = list(sems)
     loads = [
         pltpu.make_async_copy(ref, local.at[at], sems[0].at[at])
@@ -258,9 +279,10 @@
     for load in loads:
         load.start()
     rows_sems = sems[1:4]
-    swap_sems = [sems[4 + 3 * chunk : 7 + 3 * chunk] for chunk in range(CHUNKS)]
-    share_sems = [sems[4 + 3 * chunk : 7 + 3 * chunk] for chunk in range(CHUNKS, 2 * CHUNKS)]
-    greet_all(place)
+    core_send, core_recv, send_sem, recv_sem, own_sem = sems[4:9]
+    swap_sems = [sems[9 + 3 * chunk : 12 + 3 * chunk] for chunk in range(CHUNKS)]
+    share_sems = [sems[9 + 3 * chunk : 12 + 3 * chunk] for chunk in range(CHUNKS, 2 * CHUNKS)]
+    greet_all(place, zl, core)
     for load in loads:
         load.wait()
     swaps = []
@@ -279,7 +301,7 @@
         swap_wait(swaps[chunk], packed.at[chunk], moved.at[chunk], *swap_sems[chunk][:2])
         attend(moved.at[chunk], heads, grads, chunk)
         columns = pl.ds(chunk * WIDTH, WIDTH)
-        forward, finish = share_start(place[1], grads, shared, columns, *share_sems[chunk])
+        forward, finish = share_start(y, grads, shared, columns, *share_sems[chunk])
         forwards.append(forward)
         finishes.append(finish)
 
@@ -297,9 +319,77 @@
     swapped(3)
     pass_on(2)
     forwards[3]()
-    for finish in finishes:
+    for finish in finishes[:3]:
         finish()
     rows_finish()
+
+    def most(at, carry):
+        hg, slot = at // 4, at % 4
+        part[hg, pl.ds(slot * 256, 256)] = multiply(shared, rows, hg, slot, 0, 3)
+        return carry
+
+    lax.fori_loop(0, 16, most, 0)
+    finishes[3]()
+
+    halves = (1 - zl, zl)
+    copies = []
+    for at, half in enumerate(halves):
+        theirs = 2 * half + 1 - core
+
+        def last(slot, carry):
+            tokens = pl.ds(pl.multiple_of(slot * 256, 256), 256)
+            product = part[theirs, tokens] + multiply(shared, rows, theirs, slot, 3, 1)
+            leaving[at, tokens] = product.astype(BF16)
+            return carry
+
+        lax.fori_loop(0, 4, last, 0)
+        copy = pltpu.make_async_remote_copy(
+            src_ref=leaving.at[at],
+            dst_ref=other.at[at],
+            send_sem=core_send.at[at],
+            recv_sem=core_recv.at[at],
+            device_id={"c": 1 - core},
+            device_id_type=BY_MESH,
+        )
+        copy.start()
+        copies.append(copy)
+    slot_here = ((y * 4 + z) * 4 + x) * 2 + zl
+    for at, half in enumerate(halves):
+        mine = 2 * half + core
+
+        def last(slot, carry):
+            tokens = pl.ds(pl.multiple_of(slot * 256, 256), 256)
+            part[mine, tokens] += multiply(shared, rows, mine, slot, 3, 1)
+            return carry
+
+        lax.fori_loop(0, 4, last, 0)
+        copies[at].wait_recv()
+        both = part[mine] + other[at].astype(F32)
+        total[at] = pltpu.einshape("abk->bak", both.reshape(16, 64, 256)).astype(BF16)
+
+        def send(step, carry):
+            to = tm_peer(place, step)
+            pltpu.make_async_remote_copy(
+                src_ref=total.at[at, tm_index(to)],
+                dst_ref=dst.at[slot_here],
+                send_sem=send_sem,
+                recv_sem=recv_sem,
+                device_id={**to, "zl": half},
+                device_id_type=BY_MESH,
+            ).start()
+            return carry
+
+        lax.fori_loop(at, 64, send, 0)
+    own = pltpu.make_async_copy(
+        total.at[1, tm_index(tm_peer(place, 0))], dst.at[slot_here], own_sem
+    )
+    own.start()
+    rest = dst.at[pl.ds(0, 127)]
+    pltpu.make_async_copy(rest, rest, send_sem).wait()
+    pltpu.make_async_copy(rest, rest, recv_sem).wait()
+    for copy in copies:
+        copy.wait_send()
+    own.wait()
 
 
 SWAP_SEMS = [pltpu.SemaphoreType.DMA] * 3
@@ -313,122 +403,39 @@
     pltpu.SemaphoreType.DMA((4, 4)),
     pltpu.SemaphoreType.DMA,
 ]
-VMEM = pl.BlockSpec(memory_space=pltpu.VMEM)
-
-
-def params(collective_id):
-    return pltpu.CompilerParams(
-        collective_id=collective_id, has_side_effects=True, vmem_limit_bytes=32 << 20
-    )
-
-
-def front(*arrays):
+CORE_SEMS = [pltpu.SemaphoreType.DMA((2,)), pltpu.SemaphoreType.DMA((2,))]
+
+
+def whole(*arrays):
     return pl.pallas_call(
-        front_kernel,
-        out_shape=(
-            jax.ShapeDtypeStruct((3, 4, 4, 64, 1024), BF16),
-            jax.ShapeDtypeStruct((3, 16, 64, 1024), BF16),
-        ),
+        whole_kernel,
+        out_shape=jax.ShapeDtypeStruct((128, 16, 256), BF16),
         in_specs=[pl.BlockSpec(memory_space=pltpu.HBM)] * 5,
-        out_specs=(ANY, ANY),
+        out_specs=ANY,
         scratch_shapes=[
+            pltpu.VMEM((3, 4, 4, 64, 1024), BF16),
+            pltpu.VMEM((3, 16, 64, 1024), BF16),
             pltpu.VMEM((4, 256, 1024), BF16),
             pltpu.VMEM((CHUNKS, 64, 16, WIDTH), BF16),
             pltpu.VMEM((CHUNKS, 64, 16, WIDTH), BF16),
             pltpu.VMEM((16, 64, WIDTH), BF16),
             pltpu.VMEM((3, 4, 64, 1024), BF16),
+            pltpu.VMEM((4, 1024, 256), F32),
+            pltpu.VMEM((2, 1024, 256), BF16),
+            pltpu.VMEM((2, 1024, 256), BF16),
+            pltpu.VMEM((2, 64, 16, 256), BF16),
             pltpu.SemaphoreType.DMA((4,)),
             *ROWS_SEMS,
+            *CORE_SEMS,
+            *SWAP_SEMS,
             *SWAP_SEMS * CHUNKS,
             *SHARE_SEMS * CHUNKS,
         ],
-        compiler_params=params(1),
-        name="front",
-    )(*arrays)
-
-
-def deliver_kernel(part, dst, other, total, core_send, core_recv, send_sem, recv_sem, own_sem):
-    z, y, x = position()
-    zl, core = lax.axis_index("zl"), lax.axis_index("c")
-    slot = ((y * 4 + z) * 4 + x) * 2 + zl
-    barrier = pltpu.get_barrier_semaphore()
-
-    def peer(step):
-        return tm_peer((z, y, x), step)
-
-    def greet(first, half):
-        def body(step, carry):
-            pl.semaphore_signal(
-                barrier, inc=1, device_id={**peer(step), "zl": half}, device_id_type=BY_MESH
-            )
-            return carry
-
-        lax.fori_loop(first, 64, body, 0)
-
-    pl.semaphore_signal(barrier, inc=1, device_id={"c": 1 - core}, device_id_type=BY_MESH)
-    greet(0, 1 - zl)
-    greet(1, zl)
-    pl.semaphore_wait(barrier, 128)
-
-    halves = (1 - zl, zl)
-    copies = []
-    for at, half in enumerate(halves):
-        copy = pltpu.make_async_remote_copy(
-            src_ref=part.at[2 * half + 1 - core],
-            dst_ref=other.at[at],
-            send_sem=core_send.at[at],
-            recv_sem=core_recv.at[at],
-            device_id={"c": 1 - core},
-            device_id_type=BY_MESH,
-        )
-        copy.start()
-        copies.append(copy)
-    for at, half in enumerate(halves):
-        copies[at].wait_recv()
-        both = part[2 * half + core].astype(F32) + other[at].astype(F32)
-        total[at] = pltpu.einshape("abk->bak", both.reshape(16, 64, 256)).astype(BF16)
-
-        def send(step, carry):
-            to = peer(step)
-            pltpu.make_async_remote_copy(
-                src_ref=total.at[at, tm_index(to)],
-                dst_ref=dst.at[slot],
-                send_sem=send_sem,
-                recv_sem=recv_sem,
-                device_id={**to, "zl": half},
-                device_id_type=BY_MESH,
-            ).start()
-            return carry
-
-        lax.fori_loop(at, 64, send, 0)
-    own = pltpu.make_async_copy(total.at[1, z * 16 + y * 4 + x], dst.at[slot], own_sem)
-    own.start()
-    most = dst.at[pl.ds(0, 127)]
-    pltpu.make_async_copy(most, most, send_sem).wait()
-    pltpu.make_async_copy(most, most, recv_sem).wait()
-    for copy in copies:
-        copy.wait_send()
-    own.wait()
-
-
-def deliver(part):
-    return pl.pallas_call(
-        deliver_kernel,
-        out_shape=jax.ShapeDtypeStruct((128, 16, 256), part.dtype),
-        in_specs=[pl.BlockSpec(memory_space=pltpu.VMEM)],
-        out_specs=ANY,
-        scratch_shapes=[
-            pltpu.VMEM((2, 1024, 256), part.dtype),
-            pltpu.VMEM((2, 64, 16, 256), part.dtype),
-            pltpu.SemaphoreType.DMA((2,)),
-            pltpu.SemaphoreType.DMA((2,)),
-            pltpu.SemaphoreType.DMA,
-            pltpu.SemaphoreType.DMA,
-            pltpu.SemaphoreType.DMA,
-        ],
-        compiler_params=params(2),
-        name="deliver",
-    )(part)
+        compiler_params=pltpu.CompilerParams(
+            collective_id=1, has_side_effects=True, vmem_limit_bytes=56 << 20
+        ),
+        name="whole",
+    )(*(pltpu.with_memory_space_constraint(array, pltpu.HBM) for array in arrays))
 
 
 def patch_order():
@@ -437,14 +444,7 @@
 
 
 def per_device(query, key_in, value, grad_out, weights):
-    shared, rows = front(query, key_in, value, grad_out, weights)
-    partial_sum = jnp.einsum(
-        "mtk,mzik->zti",
-        shared.reshape(3, 1024, 1024),
-        rows.reshape(3, 4, 256, 1024),
-        preferred_element_type=F32,
-    )
-    back = deliver(partial_sum.astype(BF16)).reshape(4, 512, 256)
+    back = whole(query, key_in, value, grad_out, weights).reshape(4, 512, 256)
     place = jnp.asarray(patch_order(), BF16)
     out = jnp.einsum("ytk,tp->ykp", back, place, preferred_element_type=F32)
     return out.reshape(1024, 256).astype(BF16)

time: 182 us -> 170 us (0.934); the launches traced: 181 us -> 167 us
  matrix products: 8.14 us -> 1.23 us
  local copies, waits for them, and re-layouts: 5.71 us -> 1.54 us
  Pallas kernels: 167 us -> 165 us
    dot_general x1 -> x0, matrix products: 6.92 us -> none  [per_device(): jnp.einsum('mtk,mzik->zti', shared.reshape(3, 1024, 1024), rows.reshape(3...]
    unnamed x12 -> x2, local copies, waits for them, and re-layouts: 5.17 us -> 0.01 us
    pallas_call x2 -> x1, Pallas kernels: 167 us -> 165 us  [whole(): pl.pallas_call(whole_kernel, out_shape=jax.ShapeDtypeStruct((128, 16, 256...]
where the time goes in v7:
time: 170 us; the launch traced here: 167 us
  Pallas kernels  165 us (97%)
    pallas_call x1, Pallas kernels, whole(): pl.pallas_call(whole_kernel, out_shape=jax.ShapeDtypeStruct((128, 16, 256...  165 us

profile of v7, /device:TPU:1, one launch (start us, length us, event | category | flops | bytes accessed | tf_op | source)
XLA Modules:
  0.0 167.5 jit_solution(4338215166684230033)
XLA Ops:
  0.0 164.7 %whole.1 = bf16[128,16,256]{2,1,0:T(8,128)(2,1)} custom-call(bf16[256,1024]{1,0:T(8,128)(2,1)} %query.1, bf16[256,1024]{1,0:T(8,128)(2,1)} %key_in.1, bf16[256,1024]{1,0:T(8,128)(2,1)} %value.1, bf16[256,1024]{1,0:T(8,128)(2,1)} %grad_out.1, bf16[3,64,1024]{2,1,0:T(8,128)(2,1)} %own_rows.1), custom_call_target="tpu_custom_call" | custom-call | tf_op jit(solution)/shard_map/whole/pallas_call | solution.py:410
  164.7 0.0 copy-start
  164.7 1.5 copy.7
  166.3 0.0 copy-done
  166.3 1.2 convolution_convert_fusion
Async XLA Ops:
  164.7 1.6 copy-start

commit v8 on v7

--- a/solution.py
+++ b/solution.py
@@ -283,40 +283,46 @@
     swap_sems = [sems[9 + 3 * chunk : 12 + 3 * chunk] for chunk in range(CHUNKS)]
     share_sems = [sems[9 + 3 * chunk : 12 + 3 * chunk] for chunk in range(CHUNKS, 2 * CHUNKS)]
     greet_all(place, zl, core)
-    for load in loads:
-        load.wait()
     swaps = []
 
+    def pack_up(chunk):
+        pack(local, packed.at[chunk], pl.ds(chunk * WIDTH, WIDTH))
+
     def swap_out(chunk):
-        pack(local, packed.at[chunk], pl.ds(chunk * WIDTH, WIDTH))
         swaps.append(swap_start(place, packed.at[chunk], moved.at[chunk], *swap_sems[chunk]))
 
-    swap_out(0)
-    near, across, pass_on, rows_finish = rows_start(place, own_rows, rows, *rows_sems)
-    for chunk in range(1, CHUNKS):
-        swap_out(chunk)
     forwards, finishes = [], []
 
-    def swapped(chunk):
+    def swapped(chunk, following=None):
         swap_wait(swaps[chunk], packed.at[chunk], moved.at[chunk], *swap_sems[chunk][:2])
+        if following is not None:
+            swap_out(following)
         attend(moved.at[chunk], heads, grads, chunk)
         columns = pl.ds(chunk * WIDTH, WIDTH)
         forward, finish = share_start(y, grads, shared, columns, *share_sems[chunk])
         forwards.append(forward)
         finishes.append(finish)
 
-    swapped(0)
+    near, across, pass_on, rows_finish = rows_start(place, own_rows, rows, *rows_sems)
+    for load in loads:
+        load.wait()
+    pack_up(0)
+    swap_out(0)
+    for chunk in range(1, CHUNKS):
+        pack_up(chunk)
     near()
+    swap_out(1)
+    swapped(0, following=2)
     pass_on(0)
+    across()
+    swapped(1, following=3)
     forwards[0]()
-    swapped(1)
-    across()
-    forwards[1]()
     pass_on(1)
     swapped(2)
+    forwards[1]()
     pass_on(3)
+    swapped(3)
     forwards[2]()
-    swapped(3)
     pass_on(2)
     forwards[3]()
     for finish in finishes[:3]:

time: 170 us -> 177 us (1.041)
  Pallas kernels: 165 us -> 172 us
    pallas_call x1, Pallas kernels: 165 us -> 172 us  [whole(): pl.pallas_call(whole_kernel, out_shape=jax.ShapeDtypeStruct((128, 16, 256...]
where the time goes in v8:
time: 177 us; the launch traced here: 174 us
  Pallas kernels  172 us (97%)
    pallas_call x1, Pallas kernels, whole(): pl.pallas_call(whole_kernel, out_shape=jax.ShapeDtypeStruct((128, 16, 256...  172 us

profile of v8, /device:TPU:1, one launch (start us, length us, event | category | flops | bytes accessed | tf_op | source)
XLA Modules:
  0.0 174.4 jit_solution(6514443410497813753)
XLA Ops:
  0.0 171.6 %whole.1 = bf16[128,16,256]{2,1,0:T(8,128)(2,1)} custom-call(bf16[256,1024]{1,0:T(8,128)(2,1)} %query.1, bf16[256,1024]{1,0:T(8,128)(2,1)} %key_in.1, bf16[256,1024]{1,0:T(8,128)(2,1)} %value.1, bf16[256,1024]{1,0:T(8,128)(2,1)} %grad_out.1, bf16[3,64,1024]{2,1,0:T(8,128)(2,1)} %own_rows.1), custom_call_target="tpu_custom_call" | custom-call | tf_op jit(solution)/shard_map/whole/pallas_call | solution.py:416
  171.6 0.0 copy-start
  171.6 1.5 copy.7
  173.2 0.0 copy-done
  173.2 1.2 convolution_convert_fusion
Async XLA Ops:
  171.6 1.6 copy-start

commit v9 on v7

--- a/solution.py
+++ b/solution.py
@@ -1,3 +1,5 @@
+import functools
+
 import jax
 import jax.numpy as jnp
 import numpy as np
@@ -52,10 +54,15 @@
     pl.semaphore_wait(barrier, 128)
 
 
-def swap_start(place, src, dst, send_sem, recv_sem, own_sem):
+def swap_own(place, src, dst, send_sem, recv_sem, own_sem):
     me = tm_index(tm_peer(place, 0))
     own = pltpu.make_async_copy(src.at[me], dst.at[me], own_sem)
     own.start()
+    return own
+
+
+def swap_start(place, src, dst, send_sem, recv_sem, own_sem):
+    me = tm_index(tm_peer(place, 0))
 
     def send(step, carry):
         to = tm_peer(place, step)
@@ -70,7 +77,6 @@
         return carry
 
     lax.fori_loop(1, 64, send, 0)
-    return own
 
 
 def swap_wait(own, src, dst, send_sem, recv_sem):
@@ -191,8 +197,8 @@
     def block(b, at_x, part=slice(None)):
         return rows.at[:, ((z + steps[b]) % 4) * 4 + at_x, part]
 
-    def send(src, dst, axis, target, lane, b):
-        copy = pltpu.make_async_remote_copy(
+    def plan(src, dst, axis, target, lane, b):
+        return pltpu.make_async_remote_copy(
             src_ref=src,
             dst_ref=dst,
             send_sem=send_sem.at[lane, b],
@@ -200,54 +206,57 @@
             device_id={axis: target},
             device_id_type=BY_MESH,
         )
-        copy.start()
-        return copy
 
     z_up, z_down, x_up, x_down = (z + 1) % 4, (z + 3) % 4, (x + 1) % 4, (x + 3) % 4
+    low, high = pl.ds(0, 32), pl.ds(32, 32)
+    z_ups = plan(own_rows, block(0, x), "z", z_up, 0, 0)
+    z_downs = plan(own_rows, block(0, x), "z", z_down, 0, 1)
+    z_far = (
+        plan(block(1, x, low), block(1, x, low), "z", z_up, 0, 2),
+        plan(block(3, x, high), block(3, x, high), "z", z_down, 0, 3),
+    )
+    ups, downs, far = [], [], []
+    for b in range(4):
+        src = own_rows if b == 0 else block(b, x)
+        ups.append(plan(src, block(b, x), "x", x_up, 1, b))
+        downs.append(plan(src, block(b, x), "x", x_down, 2, b))
+        at, target = (x_down, x_up) if b < 2 else (x_up, x_down)
+        far.append(plan(block(b, at), block(b, at), "x", target, 3, b))
     own = pltpu.make_async_copy(own_rows, block(0, x), own_sem)
     own.start()
-    z_ups = send(own_rows, block(0, x), "z", z_up, 0, 0)
-    z_downs = send(own_rows, block(0, x), "z", z_down, 0, 1)
-    z_far, ups, downs, far = [], {}, {}, {}
-
-    def along_x(b):
-        src = own_rows if b == 0 else block(b, x)
-        ups[b] = send(src, block(b, x), "x", x_up, 1, b)
-        downs[b] = send(src, block(b, x), "x", x_down, 2, b)
-
-    along_x(0)
+    ups[0].start()
+    downs[0].start()
+
+    def along_z():
+        z_ups.start()
+        z_downs.start()
 
     def near():
-        low, high = pl.ds(0, 32), pl.ds(32, 32)
-        z_ups.wait_recv()
-        z_far.append(send(block(1, x, low), block(1, x, low), "z", z_up, 0, 2))
-        along_x(1)
-        z_downs.wait_recv()
-        z_far.append(send(block(3, x, high), block(3, x, high), "z", z_down, 0, 3))
-        along_x(3)
+        for copy, onward, b in ((z_ups, z_far[0], 1), (z_downs, z_far[1], 3)):
+            copy.wait_recv()
+            onward.start()
+            ups[b].start()
+            downs[b].start()
 
     def across():
         for copy in z_far:
             copy.wait_recv()
-        along_x(2)
+        ups[2].start()
+        downs[2].start()
 
     def forward(b):
-        if b < 2:
-            ups[b].wait_recv()
-            far[b] = send(block(b, x_down), block(b, x_down), "x", x_up, 3, b)
-        else:
-            downs[b].wait_recv()
-            far[b] = send(block(b, x_up), block(b, x_up), "x", x_down, 3, b)
+        (ups if b < 2 else downs)[b].wait_recv()
+        far[b].start()
 
     def finish():
         for b in range(4):
             (downs if b < 2 else ups)[b].wait_recv()
             far[b].wait_recv()
-        for copy in (z_ups, z_downs, *z_far, *ups.values(), *downs.values(), *far.values()):
+        for copy in (z_ups, z_downs, *z_far, *ups, *downs, *far):
             copy.wait_send()
         own.wait()
 
-    return near, across, forward, finish
+    return along_z, near, across, forward, finish
 
 
 def multiply(shared, rows, hg, slot, first_chunk, chunks):
@@ -283,19 +292,10 @@
     swap_sems = [sems[9 + 3 * chunk : 12 + 3 * chunk] for chunk in range(CHUNKS)]
     share_sems = [sems[9 + 3 * chunk : 12 + 3 * chunk] for chunk in range(CHUNKS, 2 * CHUNKS)]
     greet_all(place, zl, core)
-    for load in loads:
-        load.wait()
-    swaps = []
+    swaps, forwards, finishes = [], [], []
 
     def swap_out(chunk):
-        pack(local, packed.at[chunk], pl.ds(chunk * WIDTH, WIDTH))
-        swaps.append(swap_start(place, packed.at[chunk], moved.at[chunk], *swap_sems[chunk]))
-
-    swap_out(0)
-    near, across, pass_on, rows_finish = rows_start(place, own_rows, rows, *rows_sems)
-    for chunk in range(1, CHUNKS):
-        swap_out(chunk)
-    forwards, finishes = [], []
+        swap_start(place, packed.at[chunk], moved.at[chunk], *swap_sems[chunk])
 
     def swapped(chunk):
         swap_wait(swaps[chunk], packed.at[chunk], moved.at[chunk], *swap_sems[chunk][:2])
@@ -305,18 +305,46 @@
         forwards.append(forward)
         finishes.append(finish)
 
+    swaps_first, rows_first = pl.when(zl == 0), pl.when(zl == 1)
+    along_z, near, across, pass_on, rows_finish = rows_start(place, own_rows, rows, *rows_sems)
+    rows_first(along_z)
+    for load in loads:
+        load.wait()
+    for chunk in range(CHUNKS):
+        pack(local, packed.at[chunk], pl.ds(chunk * WIDTH, WIDTH))
+        swaps.append(swap_own(place, packed.at[chunk], moved.at[chunk], *swap_sems[chunk]))
+        swaps_first(functools.partial(swap_out, chunk))
+
+    @rows_first
+    def _():
+        near()
+        for chunk in range(CHUNKS):
+            swap_out(chunk)
+
     swapped(0)
-    near()
     pass_on(0)
+    swapped(1)
+    swaps_first(along_z)
     forwards[0]()
-    swapped(1)
-    across()
+    rows_first(across)
+    swapped(2)
     forwards[1]()
-    pass_on(1)
-    swapped(2)
-    pass_on(3)
+    swaps_first(near)
+
+    @rows_first
+    def _():
+        pass_on(1)
+        pass_on(3)
+
+    swapped(3)
     forwards[2]()
-    swapped(3)
+
+    @swaps_first
+    def _():
+        across()
+        pass_on(1)
+        pass_on(3)
+
     pass_on(2)
     forwards[3]()
     for finish in finishes[:3]:

time: 170 us -> 170 us (level)
  no operation moved by 1% of the time
where the time goes in v9:
time: 170 us; the launch traced here: 166 us
  Pallas kernels  164 us (96%)
    pallas_call x1, Pallas kernels, whole(): pl.pallas_call(whole_kernel, out_shape=jax.ShapeDtypeStruct((128, 16, 256...  164 us

profile of v9, /device:TPU:1, one launch (start us, length us, event | category | flops | bytes accessed | tf_op | source)
XLA Modules:
  0.0 166.5 jit_solution(16829470244673506579)
XLA Ops:
  0.0 163.7 %whole.1 = bf16[128,16,256]{2,1,0:T(8,128)(2,1)} custom-call(bf16[256,1024]{1,0:T(8,128)(2,1)} %query.1, bf16[256,1024]{1,0:T(8,128)(2,1)} %key_in.1, bf16[256,1024]{1,0:T(8,128)(2,1)} %value.1, bf16[256,1024]{1,0:T(8,128)(2,1)} %grad_out.1, bf16[3,64,1024]{2,1,0:T(8,128)(2,1)} %own_rows.1), custom_call_target="tpu_custom_call" | custom-call | tf_op jit(solution)/shard_map/whole/pallas_call | solution.py:438
  163.7 0.0 copy-start
  163.7 1.5 copy.7
  165.3 0.0 copy-done
  165.3 1.2 convolution_convert_fusion
Async XLA Ops:
  163.7 1.6 copy-start

commit v10 on v9

--- a/solution.py
+++ b/solution.py
@@ -24,13 +24,16 @@
     return lax.axis_index("z"), lax.axis_index("y"), lax.axis_index("x")
 
 
+def turn(at, by):
+    return lax.rem(at + by, jnp.int32(4))
+
+
 def tm_peer(place, step):
     z, y, x = place
-    return {
-        "z": (z + step // 16) % 4,
-        "y": (y + (step // 4) % 4) % 4,
-        "x": (x + step % 4) % 4,
-    }
+    step = jnp.int32(step)
+    by_x, rest = lax.rem(step, jnp.int32(4)), lax.div(step, jnp.int32(4))
+    by_y, by_z = lax.rem(rest, jnp.int32(4)), lax.div(rest, jnp.int32(4))
+    return {"z": turn(z, by_z), "y": turn(y, by_y), "x": turn(x, by_x)}
 
 
 def tm_index(at):
@@ -49,8 +52,8 @@
         return body
 
     pl.semaphore_signal(barrier, inc=1, device_id={"c": 1 - core}, device_id_type=BY_MESH)
-    lax.fori_loop(1, 64, greet(zl), 0)
-    lax.fori_loop(0, 64, greet(1 - zl), 0)
+    lax.fori_loop(1, 64, greet(zl), 0, unroll=7)
+    lax.fori_loop(0, 64, greet(1 - zl), 0, unroll=8)
     pl.semaphore_wait(barrier, 128)
 
 
@@ -76,7 +79,7 @@
         ).start()
         return carry
 
-    lax.fori_loop(1, 64, send, 0)
+    lax.fori_loop(1, 64, send, 0, unroll=7)
 
 
 def swap_wait(own, src, dst, send_sem, recv_sem):
@@ -407,7 +410,7 @@
             ).start()
             return carry
 
-        lax.fori_loop(at, 64, send, 0)
+        lax.fori_loop(at, 64, send, 0, unroll=8 - at)
     own = pltpu.make_async_copy(
         total.at[1, tm_index(tm_peer(place, 0))], dst.at[slot_here], own_sem
     )

time: 170 us -> 168 us (0.988)
  the two profiles are of different devices: /device:TPU:1 before, /device:TPU:32 now
where the time goes in v10:
time: 168 us
  Pallas kernels  165 us (98%)
    pallas_call x1, Pallas kernels, whole(): pl.pallas_call(whole_kernel, out_shape=jax.ShapeDtypeStruct((128, 16, 256...  165 us

profile of v10, /device:TPU:32, one launch (start us, length us, event | category | flops | bytes accessed | tf_op | source)
XLA Modules:
  0.0 168.2 jit_solution(11016899894371207525)
XLA Ops:
  0.0 165.4 %whole.1 = bf16[128,16,256]{2,1,0:T(8,128)(2,1)} custom-call(bf16[256,1024]{1,0:T(8,128)(2,1)} %query.1, bf16[256,1024]{1,0:T(8,128)(2,1)} %key_in.1, bf16[256,1024]{1,0:T(8,128)(2,1)} %value.1, bf16[256,1024]{1,0:T(8,128)(2,1)} %grad_out.1, bf16[3,64,1024]{2,1,0:T(8,128)(2,1)} %own_rows.1), custom_call_target="tpu_custom_call" | custom-call | tf_op jit(solution)/shard_map/whole/pallas_call | solution.py:441
  165.4 0.0 copy-start
  165.4 1.5 copy.7
  167.0 0.0 copy-done
  167.0 1.2 convolution_convert_fusion
Async XLA Ops:
  165.4 1.6 copy-start

commit v11 on v10

--- a/solution.py
+++ b/solution.py
@@ -9,8 +9,9 @@
 from jax.sharding import Mesh, PartitionSpec as P
 
 HD = 128
-CHUNKS = 4
-WIDTH = 1024 // CHUNKS
+WIDTHS = (512, 256, 256)
+STARTS = (0, 512, 768)
+CHUNKS = len(WIDTHS)
 AXES = ("z", "y", "x", "zl", "c")
 TM = AXES[:3]
 HEAD = AXES[3:]
@@ -137,24 +138,27 @@
     return forward, finish
 
 
-def pack(arrays, into, columns):
+def pack(arrays, into, start, width):
     row = lax.broadcasted_iota(jnp.int32, (64, 64), 0)
     column = lax.broadcasted_iota(jnp.int32, (64, 64), 1)
     wanted = ((row // 4) % 4) * 16 + (row // 16) * 4 + row % 4
     order = jnp.where(column == wanted, 1.0, 0.0).astype(BF16)
 
+    columns = pl.ds(start, width)
+
     def body(group, carry):
         rows = pl.ds(pl.multiple_of(group * 16, 16), 16)
         block = jnp.concatenate([arrays[at, rows, columns] for at in range(4)], axis=0)
         ordered = jnp.dot(order, block, preferred_element_type=F32).astype(BF16)
-        into[pl.ds(group * 4, 4)] = ordered.reshape(4, 16, WIDTH)
+        into[pl.ds(group * 4, 4)] = ordered.reshape(4, 16, width)
         return carry
 
     lax.fori_loop(0, 16, body, 0)
 
 
-def attend(moved, heads, grads, chunk):
-    heads[...] = pltpu.einshape("abk->bak", moved[...].astype(F32)).astype(BF16)
+def attend(moved, heads, grads, start, width):
+    turned = pltpu.einshape("abk->bak", moved[...].astype(F32))
+    heads[:, :, pl.ds(0, width)] = turned.astype(BF16)
     scale = 1.0 / HD**0.5
     row = lax.broadcasted_iota(jnp.int32, (128, 128), 0)
     column = lax.broadcasted_iota(jnp.int32, (128, 128), 1)
@@ -167,7 +171,7 @@
 
     def body(pair, carry):
         patches = pl.ds(pair * 2, 2)
-        for head in range(WIDTH // HD):
+        for head in range(width // HD):
             lanes = slice(head * HD, (head + 1) * HD)
             q, k, v, g = (
                 heads[pl.ds(array * 4 + pair * 2, 2), :, lanes].reshape(128, HD)
@@ -185,7 +189,7 @@
                 dot(grad_scores, q, 0, 0) * scale,
                 dot(probs_b, g, 0, 0),
             )
-            out = pl.ds(chunk * WIDTH + head * HD, HD)
+            out = pl.ds(start + head * HD, HD)
             for m, result in enumerate(results):
                 grads[m, patches, :, out] = result.astype(BF16).reshape(2, 64, HD)
         return carry
@@ -262,13 +266,13 @@
     return along_z, near, across, forward, finish
 
 
-def multiply(shared, rows, hg, slot, first_chunk, chunks):
-    columns = pl.ds(first_chunk * WIDTH, chunks * WIDTH)
+def multiply(shared, rows, hg, slot, start, width):
+    columns = pl.ds(start, width)
     product = None
     for m in range(3):
         term = lax.dot_general(
-            shared[m, slot, :, :, columns].reshape(256, chunks * WIDTH),
-            rows[m, pl.ds(hg * 4, 4), :, columns].reshape(256, chunks * WIDTH),
+            shared[m, slot, :, :, columns].reshape(256, width),
+            rows[m, pl.ds(hg * 4, 4), :, columns].reshape(256, width),
             (((1,), (1,)), ((), ())),
             preferred_element_type=F32,
         )
@@ -277,13 +281,13 @@
 
 
 def whole_kernel(
-    query, key_in, value, grad_out, own_rows, dst, shared, rows, local, packed, moved, heads, grads,
-    part, leaving, other, total, *sems
+    query, key_in, value, grad_out, own_rows, dst, shared, rows, local, heads, grads, part,
+    leaving, other, total, *scratch
 ):
     place = position()
     z, y, x = place
     zl, core = lax.axis_index("zl"), lax.axis_index("c")
-    sems = list(sems)
+    packed, moved, sems = scratch[:CHUNKS], scratch[CHUNKS : 2 * CHUNKS], scratch[2 * CHUNKS :]
     loads = [
         pltpu.make_async_copy(ref, local.at[at], sems[0].at[at])
         for at, ref in enumerate((query, key_in, value, grad_out))
@@ -298,12 +302,12 @@
     swaps, forwards, finishes = [], [], []
 
     def swap_out(chunk):
-        swap_start(place, packed.at[chunk], moved.at[chunk], *swap_sems[chunk])
+        swap_start(place, packed[chunk], moved[chunk], *swap_sems[chunk])
 
     def swapped(chunk):
-        swap_wait(swaps[chunk], packed.at[chunk], moved.at[chunk], *swap_sems[chunk][:2])
-        attend(moved.at[chunk], heads, grads, chunk)
-        columns = pl.ds(chunk * WIDTH, WIDTH)
+        swap_wait(swaps[chunk], packed[chunk], moved[chunk], *swap_sems[chunk][:2])
+        attend(moved[chunk], heads, grads, STARTS[chunk], WIDTHS[chunk])
+        columns = pl.ds(STARTS[chunk], WIDTHS[chunk])
         forward, finish = share_start(y, grads, shared, columns, *share_sems[chunk])
         forwards.append(forward)
         finishes.append(finish)
@@ -314,8 +318,8 @@
     for load in loads:
         load.wait()
     for chunk in range(CHUNKS):
-        pack(local, packed.at[chunk], pl.ds(chunk * WIDTH, WIDTH))
-        swaps.append(swap_own(place, packed.at[chunk], moved.at[chunk], *swap_sems[chunk]))
+        pack(local, packed[chunk], STARTS[chunk], WIDTHS[chunk])
+        swaps.append(swap_own(place, packed[chunk], moved[chunk], *swap_sems[chunk]))
         swaps_first(functools.partial(swap_out, chunk))
 
     @rows_first
@@ -326,12 +330,10 @@
 
     swapped(0)
     pass_on(0)
+    swaps_first(along_z)
+    rows_first(across)
     swapped(1)
-    swaps_first(along_z)
     forwards[0]()
-    rows_first(across)
-    swapped(2)
-    forwards[1]()
     swaps_first(near)
 
     @rows_first
@@ -339,8 +341,8 @@
         pass_on(1)
         pass_on(3)
 
-    swapped(3)
-    forwards[2]()
+    swapped(2)
+    forwards[1]()
 
     @swaps_first
     def _():
@@ -349,18 +351,18 @@
         pass_on(3)
 
     pass_on(2)
-    forwards[3]()
-    for finish in finishes[:3]:
+    forwards[2]()
+    for finish in finishes[:-1]:
         finish()
     rows_finish()
 
     def most(at, carry):
         hg, slot = at // 4, at % 4
-        part[hg, pl.ds(slot * 256, 256)] = multiply(shared, rows, hg, slot, 0, 3)
+        part[hg, pl.ds(slot * 256, 256)] = multiply(shared, rows, hg, slot, 0, STARTS[-1])
         return carry
 
     lax.fori_loop(0, 16, most, 0)
-    finishes[3]()
+    finishes[-1]()
 
     halves = (1 - zl, zl)
     copies = []
@@ -369,7 +371,7 @@
 
         def last(slot, carry):
             tokens = pl.ds(pl.multiple_of(slot * 256, 256), 256)
-            product = part[theirs, tokens] + multiply(shared, rows, theirs, slot, 3, 1)
+            product = part[theirs, tokens] + multiply(shared, rows, theirs, slot, STARTS[-1], WIDTHS[-1])
             leaving[at, tokens] = product.astype(BF16)
             return carry
 
@@ -390,7 +392,7 @@
 
         def last(slot, carry):
             tokens = pl.ds(pl.multiple_of(slot * 256, 256), 256)
-            part[mine, tokens] += multiply(shared, rows, mine, slot, 3, 1)
+            part[mine, tokens] += multiply(shared, rows, mine, slot, STARTS[-1], WIDTHS[-1])
             return carry
 
         lax.fori_loop(0, 4, last, 0)
@@ -447,14 +449,13 @@
             pltpu.VMEM((3, 4, 4, 64, 1024), BF16),
             pltpu.VMEM((3, 16, 64, 1024), BF16),
             pltpu.VMEM((4, 256, 1024), BF16),
-            pltpu.VMEM((CHUNKS, 64, 16, WIDTH), BF16),
-            pltpu.VMEM((CHUNKS, 64, 16, WIDTH), BF16),
-            pltpu.VMEM((16, 64, WIDTH), BF16),
+            pltpu.VMEM((16, 64, max(WIDTHS)), BF16),
             pltpu.VMEM((3, 4, 64, 1024), BF16),
             pltpu.VMEM((4, 1024, 256), F32),
             pltpu.VMEM((2, 1024, 256), BF16),
             pltpu.VMEM((2, 1024, 256), BF16),
             pltpu.VMEM((2, 64, 16, 256), BF16),
+            *[pltpu.VMEM((64, 16, width), BF16) for width in WIDTHS * 2],
             pltpu.SemaphoreType.DMA((4,)),
             *ROWS_SEMS,
             *CORE_SEMS,

time: 168 us -> 171 us (1.018)
  the two profiles are of different devices: /device:TPU:32 before, /device:TPU:56 now
where the time goes in v11:
time: 171 us
  Pallas kernels  168 us (98%)
    pallas_call x1, Pallas kernels, whole(): pl.pallas_call(whole_kernel, out_shape=jax.ShapeDtypeStruct((128, 16, 256...  168 us

profile of v11, /device:TPU:56, one launch (start us, length us, event | category | flops | bytes accessed | tf_op | source)
XLA Modules:
  0.0 171.0 jit_solution(11535461900962342918)
XLA Ops:
  0.0 168.2 %whole.1 = bf16[128,16,256]{2,1,0:T(8,128)(2,1)} custom-call(bf16[256,1024]{1,0:T(8,128)(2,1)} %query.1, bf16[256,1024]{1,0:T(8,128)(2,1)} %key_in.1, bf16[256,1024]{1,0:T(8,128)(2,1)} %value.1, bf16[256,1024]{1,0:T(8,128)(2,1)} %grad_out.1, bf16[3,64,1024]{2,1,0:T(8,128)(2,1)} %own_rows.1), custom_call_target="tpu_custom_call" | custom-call | tf_op jit(solution)/shard_map/whole/pallas_call | solution.py:443
  168.2 0.0 copy-start
  168.2 1.5 copy.7
  169.8 0.0 copy-done
  169.8 1.2 convolution_convert_fusion
Async XLA Ops:
  168.2 1.6 copy-start
